TPU v7x, 256 devices: a whole 4x4x8 slice. The times are simulated.
256 devices in a mesh: seq: 64 (over x, z, y_hi), dp: 4 (over y_lo, core).
Axes of the slice: x: 4, y: 4 (y_hi: 2, y_lo: 2; y = y_hi * 2 + y_lo), z: 8, core: 2. Of those that a mesh axis runs over, the one named last changes fastest.
Arguments:
- layer_input: bfloat16 [32768, 2560], P(('dp', 'seq')), may hold values from -24 to 24
- ssm_input: bfloat16 [32768, 2560], P(('dp', 'seq')), may hold values from -6 to 6
- out_grad: bfloat16 [32768, 2560], P(('dp', 'seq')), may hold values from -6 to 6
- b_weight: bfloat16 [2560, 128], replicated, may hold values from -0.125 to 0.125
- c_weight: bfloat16 [2560, 128], replicated, may hold values from -0.125 to 0.125
- dt_weight: bfloat16 [2560, 40], replicated, may hold values from -0.25 to 0.25
- dt_bias: float32 [40], replicated, may hold values from -9.7 to -8.2
- a_log: float32 [40], replicated, may hold values from -13 to 4.7
- d_skip: float32 [40], replicated, may hold values from 0.5 to 1.5
Outputs:
- grad_ssm_input: bfloat16 [32768, 2560], P(('dp', 'seq'))
- grad_layer_input: bfloat16 [32768, 2560], P(('dp', 'seq'))
- grad_b_weight: float32 [2560, 128], P('seq')
- grad_c_weight: float32 [2560, 128], P('seq')
- grad_dt_weight: float32 [2560, 40], P('seq')
- grad_dt_bias: float32 [40], replicated
- grad_a_log: float32 [40], replicated
- grad_d_skip: float32 [40], replicated
All inputs are finite; a program needn't handle non-finite values.
Results may differ from a plain program's by a relative error of at most 0.0018.
Values sent between devices are 32-bit elements; how exact they have to be, the bound alone decides.
A program may use at most 256 MiB of HBM per device.

v0:
```python
import jax
import jax.numpy as jnp
from jax import lax
from jax.sharding import Mesh
from jax.sharding import PartitionSpec as P

SEQ = ("seq_0", "seq_1", "seq_2")
SEQ_DP = ("seq_0", "seq_1", "seq_2", "dp")
DP_SEQ = ("dp", "seq_0", "seq_1", "seq_2")


EXACT = lax.Precision.HIGHEST


def nothing_yet(shard, identity):
    return jax.tree.map(
        lambda part, zero: jnp.zeros_like(part) + jnp.asarray(zero, part.dtype), shard, identity
    )


def entering(shard, axes, combine, identity, reverse):
    before = start = nothing_yet(shard, identity)
    running = shard
    for axis in reversed(axes):
        count, mine = (lax.axis_size(axis), lax.axis_index(axis))
        pieces = jax.tree.map(lambda part: lax.all_gather(part, axis), running)
        inside, running = (start, start)
        for k in reversed(range(count)) if reverse else range(count):
            passed = k > mine if reverse else k < mine
            running = combine(running, jax.tree.map(lambda part: part[k], pieces))
            inside = jax.tree.map(lambda new, old: jnp.where(passed, new, old), running, inside)
        before = combine(inside, before)
    return before


def forward_combine(earlier, later):
    return (earlier[0] + later[0], jnp.exp(later[0])[:, None, None] * earlier[1] + later[1])


def reverse_combine(earlier, later):
    return (earlier[0] + later[0], later[1] + jnp.exp(later[0])[:, None, None] * earlier[1])


def body(layer_input, ssm_input, out_grad, b_weight, c_weight, dt_weight, dt_bias, a_log, d_skip):
    length = layer_input.shape[0]
    head_count = dt_bias.shape[0]
    state_size = b_weight.shape[1]
    head_width = ssm_input.shape[1] // head_count
    proj_b = jnp.dot(layer_input, b_weight, preferred_element_type=jnp.float32)
    proj_c = jnp.dot(layer_input, c_weight, preferred_element_type=jnp.float32)
    raw_dt = jnp.dot(layer_input, dt_weight, preferred_element_type=jnp.float32) + dt_bias[None, :]
    dt_values = jax.nn.softplus(raw_dt)
    decay_rate = -jnp.exp(a_log)
    log_decay = dt_values * decay_rate[None, :]
    row_index = lax.broadcasted_iota(jnp.int32, (length, length), 0)
    col_index = lax.broadcasted_iota(jnp.int32, (length, length), 1)
    causal = row_index >= col_index
    triangle = causal.astype(jnp.float32)
    cumulative = jnp.dot(triangle, log_decay, precision=EXACT)
    block_decay = cumulative[-1]
    to_end = jnp.exp(block_decay[None, :] - cumulative)
    from_start = jnp.exp(cumulative)
    inputs = ssm_input.astype(jnp.float32).reshape(length, head_count, head_width)
    cotangent = out_grad.astype(jnp.float32).reshape(length, head_count, head_width)
    scaled_inputs = (to_end * dt_values)[:, :, None] * inputs
    scaled_cotangent = from_start[:, :, None] * cotangent
    local_state = jnp.einsum("shp,sn->hpn", scaled_inputs, proj_b, precision=EXACT)
    local_back = jnp.einsum("thp,tn->hpn", scaled_cotangent, proj_c, precision=EXACT)
    identity = (
        jnp.zeros((head_count,), jnp.float32),
        jnp.zeros((head_count, head_width, state_size), jnp.float32),
    )
    carry_in = entering((block_decay, local_state), SEQ, forward_combine, identity, False)[1]
    carry_out = entering((block_decay, local_back), SEQ, reverse_combine, identity, True)[1]
    spread = cumulative.T[:, :, None] - cumulative.T[:, None, :]
    decay_table = jnp.exp(jnp.where(causal[None], spread, -1e30))
    scores = jnp.dot(proj_c, proj_b.T, precision=EXACT)
    pair_dots = jnp.einsum("thp,shp->hts", cotangent, inputs, precision=EXACT)
    weight = decay_table * scores[None]
    back_in = jnp.einsum("hst,shp->thp", weight, cotangent, precision=EXACT)
    back_carry = jnp.einsum("hpn,tn->thp", carry_out, proj_b, precision=EXACT)
    back_in = back_in + to_end[:, :, None] * back_carry
    grad_x = dt_values[:, :, None] * back_in + d_skip[None, :, None] * cotangent
    mixed_pairs = decay_table * pair_dots
    pair_sum = jnp.einsum("hts,sh->ts", mixed_pairs, dt_values, precision=EXACT)
    grad_b = jnp.dot(pair_sum.T, proj_c, precision=EXACT)
    grad_b = grad_b + jnp.einsum("thp,hpn->tn", scaled_inputs, carry_out, precision=EXACT)
    grad_c = jnp.dot(pair_sum, proj_b, precision=EXACT)
    grad_c = grad_c + jnp.einsum("thp,hpn->tn", scaled_cotangent, carry_in, precision=EXACT)
    pair_terms = weight * pair_dots * dt_values.T[:, None, :]
    front_carry = jnp.einsum("hpn,tn->thp", carry_in, proj_c, precision=EXACT)
    own_in = from_start * jnp.sum(cotangent * front_carry, axis=2)
    own_out = to_end * dt_values * jnp.sum(inputs * back_carry, axis=2)
    cross_term = jnp.exp(block_decay) * jnp.sum(carry_out * carry_in, axis=(1, 2))
    last_row = (lax.broadcasted_iota(jnp.int32, (length, 1), 0) == length - 1).astype(jnp.float32)
    change = jnp.sum(pair_terms, axis=2).T - jnp.sum(pair_terms, axis=1).T + own_in - own_out
    change = change + last_row * (cross_term + jnp.sum(own_out, axis=0))[None, :]
    grad_log = jnp.dot(triangle.T, change, precision=EXACT)
    direct = jnp.sum(inputs * back_in, axis=2)
    grad_raw = (direct + grad_log * decay_rate[None, :]) * jax.nn.sigmoid(raw_dt)
    grad_bias = jnp.sum(grad_raw, axis=0)
    grad_alog = jnp.sum(grad_log * dt_values, axis=0) * decay_rate
    grad_skip = jnp.sum(cotangent * inputs, axis=(0, 2))
    extras = jnp.stack([grad_bias, grad_alog, grad_skip])
    grad_cols = jnp.concatenate([grad_b, grad_c, grad_raw], axis=1)
    weights_wide = jnp.concatenate([b_weight, c_weight, dt_weight], axis=1).astype(jnp.float32)
    grad_u = jnp.dot(grad_cols, weights_wide.T, precision=EXACT).astype(jnp.bfloat16)
    u_wide = layer_input.astype(jnp.float32)
    row_count = layer_input.shape[1] // lax.axis_size(SEQ)
    full_grads = jnp.einsum("td,tk->dk", u_wide, grad_cols, precision=EXACT)
    summed, small_grads = lax.psum((full_grads, extras), SEQ_DP)
    row_grads = lax.dynamic_slice_in_dim(summed, lax.axis_index(SEQ) * row_count, row_count, 0)
    grad_x_out = grad_x.reshape(length, head_count * head_width).astype(jnp.bfloat16)
    return (
        grad_x_out,
        grad_u,
        row_grads[:, :state_size],
        row_grads[:, state_size : 2 * state_size],
        row_grads[:, 2 * state_size :],
        small_grads[0],
        small_grads[1],
        small_grads[2],
    )


def solution(mesh):
    split = Mesh(mesh.devices.reshape(4, 8, 2, mesh.shape["dp"]), ("seq_0", "seq_1", "seq_2", "dp"))
    placed = (P(DP_SEQ, None), P(DP_SEQ, None), P(DP_SEQ, None), P(), P(), P(), P(), P(), P())
    return jax.shard_map(
        body,
        mesh=split,
        in_specs=placed,
        out_specs=(
            P(DP_SEQ, None),
            P(DP_SEQ, None),
            P(SEQ, None),
            P(SEQ, None),
            P(SEQ, None),
            P(),
            P(),
            P(),
        ),
        check_vma=False,
    )
```

profile of v0, /device:TPU:1, one launch (start us, length us, event | category | flops | bytes accessed | tf_op | source)
XLA Modules:
  0.0 777.7 jit_solution(11077945180954140211)
XLA Ops:
  8.3 1.9 compare_select_fusion
  10.6 1.4 fusion.226
  13.0 2.3 fusion.57
  16.7 2.3 fusion.84
  19.1 5.3 all-gather.2
  25.0 40.0 %all-gather.23.cloned.1.call-done = f32[80,64,128]{2,1,0:T(8,128)} async-done(((f32[40,64,128]{2,1,0:T(8,128)}), f32[80,64,128]{2,1,0:T(8,128)}) %all-gather.23.cloned.1.call-update) | async-done | bytes 2621456 | tf_op jit(solution)/shard_map/all_gather | solution.py:26
  64.9 3.0 bitcast_add_fusion.12
  68.1 43.8 %all-gather.21.cloned.1.call-done = f32[80,64,128]{2,1,0:T(8,128)} async-done(((f32[40,64,128]{2,1,0:T(8,128)}), f32[80,64,128]{2,1,0:T(8,128)}) %all-gather.21.cloned.1.call-update) | async-done | bytes 2621456 | tf_op jit(solution)/shard_map/all_gather | solution.py:26
  111.8 3.0 bitcast_add_fusion.27
  115.0 12.7 %all-gather.3 = f32[8,1,40]{2,1,0:T(1,128)S(1)} all-gather(f32[1,1,40]{2,1,0:T(1,128)S(1)} %get-tuple-element.107), channel_id=1, replica_groups=mesh['seq_0'=4,'seq_1'=8,'seq_2'=2,'dp'=4] {'seq_1'}, dimensions={0}, use_global_device_ids=true | all-gather | bytes 1440 | tf_op jit(solution)/shard_map/all_gather | solution.py:26
  128.3 98.6 %all-gather.17.cloned.1.call-done = f32[8,40,64,128]{3,2,1,0:T(8,128)} async-done(((f32[1,40,64,128]{3,2,1,0:T(8,128)}), f32[8,40,64,128]{3,2,1,0:T(8,128)}) %all-gather.17.cloned.1.call-update) | async-done | bytes 10485776 | tf_op jit(solution)/shard_map/all_gather | solution.py:26
  226.9 5.9 multiply_add_fusion
  232.9 108.0 %all-gather.13.cloned.1.call-done = f32[8,40,64,128]{3,2,1,0:T(8,128)} async-done(((f32[1,40,64,128]{3,2,1,0:T(8,128)}), f32[8,40,64,128]{3,2,1,0:T(8,128)}) %all-gather.13.cloned.1.call-update) | async-done | bytes 10485776 | tf_op jit(solution)/shard_map/all_gather | solution.py:26
  341.0 5.9 multiply_add_fusion.7
  347.1 2.4 multiply_reduce_fusion.1
  350.6 7.6 all-gather.4
  358.2 6.0 all-gather.5
  366.2 2.7 fusion.8
  368.9 1.2 multiply_reduce_fusion
  370.1 30.7 %all-gather.19.cloned.1.call-done = f32[4,40,64,128]{3,2,1,0:T(8,128)} async-done(((f32[1,40,64,128]{3,2,1,0:T(8,128)}), f32[4,40,64,128]{3,2,1,0:T(8,128)}) %all-gather.19.cloned.1.call-update) | async-done | bytes 5242896 | tf_op jit(solution)/shard_map/all_gather | solution.py:26
  400.8 61.7 %all-gather.15.cloned.1.call-done = f32[4,40,64,128]{3,2,1,0:T(8,128)} async-done(((f32[1,40,64,128]{3,2,1,0:T(8,128)}), f32[4,40,64,128]{3,2,1,0:T(8,128)}) %all-gather.15.cloned.1.call-update) | async-done | bytes 5242896 | tf_op jit(solution)/shard_map/all_gather | solution.py:26
  462.5 13.0 %multiply_reduce_fusion.2 = (f32[40]{0:T(128)S(1)}, f32[40,64,128]{2,1,0:T(8,128)S(1)}, f32[40,64,128]{2,1,0:T(8,128)S(1)}) fusion(pred[]{:T(512)S(6)} %gt.51, f32[80,64,128]{2,1,0:T(8,128)S(1)} %copy-done.1, f32[40]{0:T(128)} %copy-done.46, f32[40]{0:T(128)} %copy-done.57, pred[]{:T(512)S(6)} %gt.50, pred[]{:T(512)S(6)} %gt.49, pred[]{:T(512)S(6)} %gt.48, ...), kind=kLoop, calls=%fused_computation.64 | loop fusion | flops 28835800 | bytes 39325948 | tf_op jit(solution)/shard_map/reduce_sum | solution.py:94
  475.5 1.2 fusion.91
  476.9 1.2 fusion.165
  478.2 3.3 multiply_reduce_fusion.3
  481.9 7.8 %fusion.102 = f32[128,128]{0,1:T(8,128)S(1)} fusion(f32[128,40,64]{0,2,1:T(8,128)S(1)} %bitcast.436, f32[1,40,64,128]{3,2,1,0:T(8,128)S(1)} %copy-done.8, f32[1,40,64,128]{3,2,1,0:T(8,128)S(1)} %copy-done.12, f32[1,40,64,128]{3,2,1,0:T(8,128)S(1)} %copy-done.10, f32[4,40,64,128]{3,2,1,0:T(8,128)} %all-gather.15.cloned.1.call-done, ...), kind=kOutput, calls=%fused_computation.154 | convolution fusion | flops 515440640 | bytes 19733006 | tf_op jit(solution)/shard_map/thp,hpn->tn/dot_general | solution.py:87
  490.1 7.9 %fusion.105 = f32[128,128]{0,1:T(8,128)S(1)} fusion(f32[128,40,64]{0,2,1:T(8,128)S(1)} %bitcast.435, f32[1,40,64,128]{3,2,1,0:T(8,128)S(1)} %copy-done.9, f32[1,40,64,128]{3,2,1,0:T(8,128)S(1)} %copy-done.7, f32[1,40,64,128]{3,2,1,0:T(8,128)S(1)} %copy-done.11, f32[4,40,64,128]{3,2,1,0:T(8,128)} %all-gather.19.cloned.1.call-done, ...), kind=kOutput, calls=%fused_computation.155 | convolution fusion | flops 515440640 | bytes 19733006 | tf_op jit(solution)/shard_map/thp,hpn->tn/dot_general | solution.py:89
  499.3 3.0 convolution_bitcast_fusion
  504.4 1.1 copy.72
  506.2 77.2 %psum.15 = f32[3,40]{1,0:T(4,128)S(1)} all-reduce(f32[3,40]{1,0:T(4,128)S(1)} %pad_maximum_fusion.3), channel_id=1, replica_groups=mesh['seq_0'=4,'seq_1'=8,'seq_2'=2,'dp'=4] {'seq_0','seq_1','seq_2','dp'}, use_global_device_ids=true, to_apply=%region_12.13 | all-reduce | flops 120 | bytes 960 | tf_op jit(solution)/shard_map/psum | solution.py:111
  583.5 3.0 convolution_convert_fusion
  587.0 179.9 %all-reduce.2.cloned.1.call-done = f32[2560,296]{0,1:T(8,128)} async-done(((f32[2560,296]{0,1:T(8,128)}), f32[2560,296]{0,1:T(8,128)}) %all-reduce.2.cloned.1.call-update) | async-done | bytes 3031056 | tf_op jit(solution)/shard_map/psum | solution.py:111
  (198 shorter events, 17.5 us)
Async XLA Ops:
  7.2 57.7 %all-gather.23.cloned.1.call-start = ((), (), s32[]{:S(2)}) async-start(), calls=%async_computation.6 | async-start | bytes 3932160 | tf_op jit(solution)/shard_map/all_gather | solution.py:26
  13.0 353.2 %copy-start.5 = (bf16[128,2560]{0,1:T(8,128)(2,1)}, bf16[128,2560]{0,1:T(8,128)(2,1)S(1)}, u32[]{:S(2)}) copy-start(bf16[128,2560]{0,1:T(8,128)(2,1)S(1)} %copy.69) | copy-start | bytes 1966084
  15.3 96.5 %all-gather.21.cloned.1.call-start = ((), (), s32[]{:S(2)}) async-start(), calls=%async_computation.5 | async-start | bytes 3932160 | tf_op jit(solution)/shard_map/all_gather | solution.py:26
  16.4 349.8 %copy-start.3 = (bf16[128,2560]{0,1:T(8,128)(2,1)}, bf16[128,2560]{0,1:T(8,128)(2,1)S(1)}, u32[]{:S(2)}) copy-start(bf16[128,2560]{0,1:T(8,128)(2,1)S(1)} %copy.66) | copy-start | bytes 1966084
  19.0 207.9 %all-gather.17.cloned.1.call-start = ((), (), s32[]{:S(2)}) async-start(), calls=%async_computation.2 | async-start | bytes 11796480 | tf_op jit(solution)/shard_map/all_gather | solution.py:26
  24.4 43.5 %copy-start.57 = (f32[40]{0:T(128)}, f32[40]{0:T(128)S(1)}, u32[]{:S(2)}) copy-start(f32[40]{0:T(128)S(1)} %get-tuple-element.102) | copy-start | bytes 484
  24.4 87.4 %copy-start.56 = (f32[40]{0:T(128)}, f32[40]{0:T(128)S(1)}, u32[]{:S(2)}) copy-start(f32[40]{0:T(128)S(1)} %get-tuple-element.101) | copy-start | bytes 484
  25.0 43.0 %copy-start.46 = (f32[40]{0:T(128)}, f32[40]{0:T(128)S(1)}, u32[]{:S(2)}) copy-start(f32[40]{0:T(128)S(1)} %get-tuple-element.104) | copy-start | bytes 484
  25.0 86.9 %copy-start.48 = (f32[40]{0:T(128)}, f32[40]{0:T(128)S(1)}, u32[]{:S(2)}) copy-start(f32[40]{0:T(128)S(1)} %get-tuple-element.103) | copy-start | bytes 484
  68.0 273.0 %all-gather.13.cloned.1.call-start = ((), (), s32[]{:S(2)}) async-start(), calls=%async_computation | async-start | bytes 11796480 | tf_op jit(solution)/shard_map/all_gather | solution.py:26
  114.9 285.9 %all-gather.19.cloned.1.call-start = ((), (), s32[]{:S(2)}) async-start(), calls=%async_computation.3 | async-start | bytes 6553600 | tf_op jit(solution)/shard_map/all_gather | solution.py:26
  128.2 104.6 %copy-start.50 = (f32[40]{0:T(128)}, f32[40]{0:T(128)S(1)}, u32[]{:S(2)}) copy-start(f32[40]{0:T(128)S(1)} %get-tuple-element.78) | copy-start | bytes 484
  128.2 212.7 %copy-start.52 = (f32[40]{0:T(128)}, f32[40]{0:T(128)S(1)}, u32[]{:S(2)}) copy-start(f32[40]{0:T(128)S(1)} %get-tuple-element.79) | copy-start | bytes 484
  128.3 104.6 %copy-start.55 = (f32[40]{0:T(128)}, f32[40]{0:T(128)S(1)}, u32[]{:S(2)}) copy-start(f32[40]{0:T(128)S(1)} %get-tuple-element.87) | copy-start | bytes 484
  128.3 212.7 %copy-start.34 = (f32[40]{0:T(128)}, f32[40]{0:T(128)S(1)}, u32[]{:S(2)}) copy-start(f32[40]{0:T(128)S(1)} %get-tuple-element.81) | copy-start | bytes 484
  128.3 212.7 %copy-start.36 = (f32[40]{0:T(128)}, f32[40]{0:T(128)S(1)}, u32[]{:S(2)}) copy-start(f32[40]{0:T(128)S(1)} %get-tuple-element.82) | copy-start | bytes 484
  128.3 212.7 %copy-start.38 = (f32[40]{0:T(128)}, f32[40]{0:T(128)S(1)}, u32[]{:S(2)}) copy-start(f32[40]{0:T(128)S(1)} %get-tuple-element.83) | copy-start | bytes 484
  128.3 212.7 %copy-start.40 = (f32[40]{0:T(128)}, f32[40]{0:T(128)S(1)}, u32[]{:S(2)}) copy-start(f32[40]{0:T(128)S(1)} %get-tuple-element.85) | copy-start | bytes 484
  128.3 212.7 %copy-start.42 = (f32[40]{0:T(128)}, f32[40]{0:T(128)S(1)}, u32[]{:S(2)}) copy-start(f32[40]{0:T(128)S(1)} %get-tuple-element.86) | copy-start | bytes 484
  128.3 212.7 %copy-start.44 = (f32[40]{0:T(128)}, f32[40]{0:T(128)S(1)}, u32[]{:S(2)}) copy-start(f32[40]{0:T(128)S(1)} %get-tuple-element.84) | copy-start | bytes 484
  128.3 212.7 %copy-start.54 = (f32[40]{0:T(128)}, f32[40]{0:T(128)S(1)}, u32[]{:S(2)}) copy-start(f32[40]{0:T(128)S(1)} %get-tuple-element.80) | copy-start | bytes 484
  232.9 229.6 %all-gather.15.cloned.1.call-start = ((), (), s32[]{:S(2)}) async-start(), calls=%async_computation.1 | async-start | bytes 6553600 | tf_op jit(solution)/shard_map/all_gather | solution.py:26
  347.0 419.9 %all-reduce.2.cloned.1.call-start = ((), (), s32[]{:S(2)}) async-start(), calls=%async_computation.4 | async-start | bytes 6062080 | tf_op jit(solution)/shard_map/psum | solution.py:111
  347.1 19.2 %copy-start.33 = (f32[40,128]{1,0:T(8,128)S(1)}, f32[40,128]{1,0:T(8,128)}, u32[]{:S(2)}) copy-start(f32[40,128]{1,0:T(8,128)} %get-tuple-element.108) | copy-start | bytes 61444
  368.9 93.6 %copy-start.1 = (f32[80,64,128]{2,1,0:T(8,128)S(1)}, f32[80,64,128]{2,1,0:T(8,128)}, u32[]{:S(2)}) copy-start(f32[80,64,128]{2,1,0:T(8,128)} %all-gather.23.cloned.1.call-done) | copy-start | bytes 7864324
  462.5 13.1 %copy-start.4 = (bf16[128,2560]{0,1:T(8,128)(2,1)S(1)}, bf16[128,2560]{0,1:T(8,128)(2,1)}, u32[]{:S(2)}) copy-start(bf16[128,2560]{0,1:T(8,128)(2,1)} %copy-done.3) | copy-start | bytes 1966084
  490.0 9.3 %copy-start.22 = (f32[128,128]{0,1:T(8,128)}, f32[128,128]{0,1:T(8,128)S(1)}, u32[]{:S(2)}) copy-start(f32[128,128]{0,1:T(8,128)S(1)} %convolution_add_fusion.1) | copy-start | bytes 196612
  502.3 81.2 %copy-start.18 = (bf16[2560,128]{1,0:T(8,128)(2,1)S(1)}, bf16[2560,128]{1,0:T(8,128)(2,1)}, u32[]{:S(2)}) copy-start(bf16[2560,128]{1,0:T(8,128)(2,1)} %param.12) | copy-start | bytes 1966084
  502.3 81.2 %copy-start.20 = (bf16[2560,128]{1,0:T(8,128)(2,1)S(1)}, bf16[2560,128]{1,0:T(8,128)(2,1)}, u32[]{:S(2)}) copy-start(bf16[2560,128]{1,0:T(8,128)(2,1)} %param.13) | copy-start | bytes 1966084
  502.3 81.2 %copy-start.23 = (f32[128,128]{0,1:T(8,128)S(1)}, f32[128,128]{0,1:T(8,128)}, u32[]{:S(2)}) copy-start(f32[128,128]{0,1:T(8,128)} %copy-done.22) | copy-start | bytes 196612
  503.5 80.0 %copy-start.25 = (f32[128,128]{0,1:T(8,128)S(1)}, f32[128,128]{0,1:T(8,128)}, u32[]{:S(2)}) copy-start(f32[128,128]{0,1:T(8,128)} %copy-done.24) | copy-start | bytes 196612
  503.5 80.0 %copy-start.31 = (f32[128,40]{0,1:T(8,128)S(1)}, f32[128,40]{0,1:T(8,128)}, u32[]{:S(2)}) copy-start(f32[128,40]{0,1:T(8,128)} %copy-done.30) | copy-start | bytes 61444
  (49 other events, 232.1 us)
Sparse Core Ops, SparseCore 0:
  15.5 49.4 all-gather.22
  66.7 45.0 all-gather.20
  113.6 113.2 all-gather.16
  228.6 112.3 all-gather.12
  342.6 58.0 all-gather.18
  402.4 60.0 all-gather.14
  502.4 264.4 all-reduce.1
where the time goes:
time: 779 us; the launch traced here: 778 us
  waiting for transfers between devices  563 us (72%)
  blocking collectives  109 us (14%)
  other arithmetic  40.2 us (5%)
  matrix products  40.1 us (5%)
  between operations  15.2 us (2%)
  local copies, waits for them, and re-layouts  10.2 us (1%)
    all_gather x6, waiting for transfers between devices, entering(): pieces = jax.tree.map(lambda part: lax.all_gather(part, axis), running)  383 us
    psum x1, waiting for transfers between devices, body(): summed, small_grads = lax.psum((full_grads, extras), SEQ_DP)  180 us
    psum x1, blocking collectives, body(): summed, small_grads = lax.psum((full_grads, extras), SEQ_DP)  77.2 us
    all_gather x4, blocking collectives, entering(): pieces = jax.tree.map(lambda part: lax.all_gather(part, axis), running)  31.6 us
  transfers between devices with their start and end apart: 7, of which 7 were waited for; matrix products, arithmetic and copies ran while one was open for 5% of the time, Pallas kernels for 0%

commit v1 on v0

--- a/solution.py
+++ b/solution.py
@@ -1,44 +1,411 @@
 import jax
 import jax.numpy as jnp
 from jax import lax
+from jax.experimental import pallas as pl
+from jax.experimental.pallas import tpu as pltpu
 from jax.sharding import Mesh
 from jax.sharding import PartitionSpec as P
 
-SEQ = ("seq_0", "seq_1", "seq_2")
-SEQ_DP = ("seq_0", "seq_1", "seq_2", "dp")
-DP_SEQ = ("dp", "seq_0", "seq_1", "seq_2")
-
-
+SEQ = ("x", "z", "yh")
+DP_SEQ = ("yl", "core", "x", "z", "yh")
 EXACT = lax.Precision.HIGHEST
 
-
-def nothing_yet(shard, identity):
-    return jax.tree.map(
-        lambda part, zero: jnp.zeros_like(part) + jnp.asarray(zero, part.dtype), shard, identity
+AXES = ("x", "z", "yh", "yl", "core")
+SIZES = {"x": 4, "z": 8, "yh": 2, "yl": 2, "core": 2}
+MESH = pl.DeviceIdType.MESH
+HEADS, WIDTH, STATE = 40, 64, 128
+HALF = HEADS // 2
+CHUNK = 4
+CHUNKS = HALF // CHUNK
+NX, NZ = SIZES["x"], SIZES["z"]
+PIECE = WIDTH // NZ
+
+
+def place():
+    return {axis: lax.axis_index(axis) for axis in AXES}
+
+
+def shifted(here, **steps):
+    there = dict(here)
+    for axis, step in steps.items():
+        there[axis] = lax.rem(here[axis] + step, SIZES[axis])
+    return tuple(there[axis] for axis in AXES)
+
+
+def greet(peers):
+    barrier = pltpu.get_barrier_semaphore()
+    for peer in peers:
+        pl.semaphore_signal(barrier, inc=1, device_id=peer, device_id_type=MESH)
+    pl.semaphore_wait(barrier, len(peers))
+
+
+def push(src, dst, send, recv, peer):
+    return pltpu.make_async_remote_copy(
+        src_ref=src, dst_ref=dst, send_sem=send, recv_sem=recv, device_id=peer, device_id_type=MESH
     )
 
 
-def entering(shard, axes, combine, identity, reverse):
-    before = start = nothing_yet(shard, identity)
-    running = shard
-    for axis in reversed(axes):
-        count, mine = (lax.axis_size(axis), lax.axis_index(axis))
-        pieces = jax.tree.map(lambda part: lax.all_gather(part, axis), running)
-        inside, running = (start, start)
-        for k in reversed(range(count)) if reverse else range(count):
-            passed = k > mine if reverse else k < mine
-            running = combine(running, jax.tree.map(lambda part: part[k], pieces))
-            inside = jax.tree.map(lambda new, old: jnp.where(passed, new, old), running, inside)
-        before = combine(inside, before)
-    return before
-
-
-def forward_combine(earlier, later):
-    return (earlier[0] + later[0], jnp.exp(later[0])[:, None, None] * earlier[1] + later[1])
-
-
-def reverse_combine(earlier, later):
-    return (earlier[0] + later[0], later[1] + jnp.exp(later[0])[:, None, None] * earlier[1])
+def scan_kernel(
+    sr, dec, out, par, pq, arec, xs, xr, bs, ps, ys, dpar, coef, pair, zd, rd,
+    y1s, y1r, as_, ar_, xss, xrs, bss, brs, y2s, y2r, d1s, d1r, d2s, d2r, d3s, d3r,
+):
+    here = place()
+    x, z, h = here["x"], here["z"], here["yh"]
+    low = h == 0
+    mine, other = h * HALF, (1 - h) * HALF
+    partner = shifted(here, yh=1)
+    zpeers = [shifted(here, z=d) for d in range(1, NZ)]
+    xpeers = [shifted(here, x=d) for d in range(1, NX)]
+    greet([partner] + zpeers + xpeers)
+
+    first = push(dec.at[1 - h], dpar, d1s, d1r, partner)
+    first.start()
+    y1 = [
+        push(
+            sr.at[:, pl.ds(other + c * CHUNK, CHUNK)],
+            par.at[:, pl.ds(c * CHUNK, CHUNK)],
+            y1s.at[c], y1r.at[c], partner,
+        )
+        for c in range(CHUNKS)
+    ]
+    y1[0].start()
+    y1[1].start()
+    xr[x] = jnp.zeros((HALF, PIECE, STATE), jnp.float32)
+    first.wait()
+    own_decay = dec[h]
+    par_decay = dpar[...]
+    one = jnp.ones_like(own_decay)
+    coef[0] = jnp.where(low, par_decay, one)
+    coef[1] = jnp.where(low, one, own_decay)
+    coef[2] = jnp.where(low, one, par_decay)
+    coef[3] = jnp.where(low, own_decay, one)
+    pair[...] = own_decay * par_decay
+    zd[z] = own_decay * par_decay
+    second = [
+        push(pair, zd.at[z], d2s.at[d], d2r.at[d], peer) for d, peer in enumerate(zpeers)
+    ]
+    for copy in second:
+        copy.start()
+    for copy in second:
+        copy.wait()
+    row = zd[0]
+    for k in range(1, NZ):
+        row = row * zd[k]
+    rd[x] = row
+    third = [push(rd.at[x], rd.at[x], d3s.at[d], d3r.at[d], peer) for d, peer in enumerate(xpeers)]
+    for copy in third:
+        copy.start()
+
+    def a_copies(c):
+        heads = pl.ds(c * CHUNK, CHUNK)
+        copies = []
+        for d, peer in enumerate(zpeers):
+            pz = pl.multiple_of(lax.rem(z + d + 1, NZ) * PIECE, PIECE)
+            copies.append(
+                push(pq.at[:, heads, pl.ds(pz, PIECE)], arec.at[z, :, heads], as_.at[c, d], ar_.at[c, d], peer)
+            )
+        return copies
+
+    def x_copies(c):
+        heads = pl.ds(c * CHUNK, CHUNK)
+        copies = []
+        for d, peer in enumerate(xpeers):
+            px = lax.rem(x + d + 1, NX)
+            back = jnp.where(px > x, 0, 1)
+            copies.append(push(xs.at[back, heads], xr.at[x, heads], xss.at[c, d], xrs.at[c, d], peer))
+        return copies
+
+    def b_copies(c):
+        heads = pl.ds(c * CHUNK, CHUNK)
+        here_rows = pl.ds(pl.multiple_of(z * PIECE, PIECE), PIECE)
+        copies = []
+        for d, peer in enumerate(zpeers):
+            pz = lax.rem(z + d + 1, NZ)
+            copies.append(
+                push(bs.at[pz, :, heads], ps.at[:, heads, here_rows], bss.at[c, d], brs.at[c, d], peer)
+            )
+        return copies
+
+    def y2_copy(c):
+        return push(
+            ys.at[:, pl.ds(c * CHUNK, CHUNK)],
+            out.at[:, pl.ds(mine + c * CHUNK, CHUNK)],
+            y2s.at[c], y2r.at[c], partner,
+        )
+
+    def pairs(c):
+        y1[c].wait_recv()
+        if c + 2 < CHUNKS:
+            y1[c + 2].start()
+
+        def head(i, carry):
+            k = c * CHUNK + i
+            at = pl.ds(k, 1)
+            pq[0, k] = coef[0, at, :] * sr[0, mine + k] + coef[1, at, :] * par[0, k]
+            pq[1, k] = coef[2, at, :] * sr[1, mine + k] + coef[3, at, :] * par[1, k]
+            return carry
+
+        lax.fori_loop(0, CHUNK, head, 0)
+        heads = pl.ds(c * CHUNK, CHUNK)
+        own = pl.ds(pl.multiple_of(z * PIECE, PIECE), PIECE)
+        arec[z, :, heads] = pq[:, heads, own, :]
+        for copy in a_copies(c):
+            copy.start()
+
+    def totals(c):
+        for copy in a_copies(c):
+            copy.wait_recv()
+
+        def head(i, carry):
+            k = c * CHUNK + i
+            at = pl.ds(k, 1)
+            forward = arec[0, 0, k]
+            backward = arec[NZ - 1, 1, k]
+            for j in range(1, NZ):
+                forward = zd[j, at, :] * forward + arec[j, 0, k]
+                backward = zd[NZ - 1 - j, at, :] * backward + arec[NZ - 1 - j, 1, k]
+            xs[0, k] = forward
+            xs[1, k] = backward
+            return carry
+
+        lax.fori_loop(0, CHUNK, head, 0)
+        for copy in x_copies(c):
+            copy.start()
+
+    def prefixes(c):
+        if c == 0:
+            for copy in third:
+                copy.wait()
+        for copy in x_copies(c):
+            copy.wait_recv()
+
+        def head(i, carry):
+            k = c * CHUNK + i
+            at = pl.ds(k, 1)
+            forward = jnp.zeros((PIECE, STATE), jnp.float32)
+            backward = jnp.zeros((PIECE, STATE), jnp.float32)
+            for j in range(NX):
+                forward = jnp.where(j < x, rd[j, at, :] * forward + xr[j, k], forward)
+                m = NX - 1 - j
+                backward = jnp.where(m > x, rd[m, at, :] * backward + xr[m, k], backward)
+            for j in range(NZ):
+                bs[j, 0, k] = forward
+                forward = zd[j, at, :] * forward + arec[j, 0, k]
+                m = NZ - 1 - j
+                bs[m, 1, k] = backward
+                backward = zd[m, at, :] * backward + arec[m, 1, k]
+            return carry
+
+        lax.fori_loop(0, CHUNK, head, 0)
+        heads = pl.ds(c * CHUNK, CHUNK)
+        own = pl.ds(pl.multiple_of(z * PIECE, PIECE), PIECE)
+        ps[:, heads, own, :] = bs[z, :, heads]
+        for copy in b_copies(c):
+            copy.start()
+
+    def finals(c):
+        for copy in b_copies(c):
+            copy.wait_recv()
+
+        def head(i, carry):
+            k = c * CHUNK + i
+            at = pl.ds(k, 1)
+            before, after = ps[0, k], ps[1, k]
+            zero = jnp.zeros_like(before)
+            ys[0, k] = coef[3, at, :] * before + jnp.where(low, sr[0, mine + k], zero)
+            ys[1, k] = coef[1, at, :] * after + jnp.where(low, zero, sr[1, mine + k])
+            out[0, mine + k] = coef[2, at, :] * before + jnp.where(low, zero, par[0, k])
+            out[1, mine + k] = coef[0, at, :] * after + jnp.where(low, par[1, k], zero)
+            return carry
+
+        lax.fori_loop(0, CHUNK, head, 0)
+        y2_copy(c).start()
+
+    for step in range(CHUNKS + 3):
+        if step < CHUNKS:
+            pairs(step)
+        if 0 <= step - 1 < CHUNKS:
+            totals(step - 1)
+        if 0 <= step - 2 < CHUNKS:
+            prefixes(step - 2)
+        if 0 <= step - 3 < CHUNKS:
+            finals(step - 3)
+    for c in range(CHUNKS):
+        y2_copy(c).wait_recv()
+    for c in range(CHUNKS):
+        y1[c].wait_send()
+        for copy in a_copies(c) + x_copies(c) + b_copies(c):
+            copy.wait_send()
+        y2_copy(c).wait_send()
+
+
+def scan_states(states, decay):
+    vmem = pl.BlockSpec(memory_space=pltpu.VMEM)
+    f32 = jnp.float32
+    dma = pltpu.SemaphoreType.DMA
+    half = (2, HALF, WIDTH, STATE)
+    return pl.pallas_call(
+        scan_kernel,
+        out_shape=jax.ShapeDtypeStruct(states.shape, f32),
+        in_specs=[vmem, vmem],
+        out_specs=vmem,
+        scratch_shapes=[
+            pltpu.VMEM(half, f32),
+            pltpu.VMEM(half, f32),
+            pltpu.VMEM((NZ, 2, HALF, PIECE, STATE), f32),
+            pltpu.VMEM((2, HALF, PIECE, STATE), f32),
+            pltpu.VMEM((NX, HALF, PIECE, STATE), f32),
+            pltpu.VMEM((NZ, 2, HALF, PIECE, STATE), f32),
+            pltpu.VMEM(half, f32),
+            pltpu.VMEM(half, f32),
+            pltpu.VMEM((24, STATE), f32),
+            pltpu.VMEM((4, 24, STATE), f32),
+            pltpu.VMEM((24, STATE), f32),
+            pltpu.VMEM((NZ, 24, STATE), f32),
+            pltpu.VMEM((NX, 24, STATE), f32),
+            dma((CHUNKS,)), dma((CHUNKS,)),
+            dma((CHUNKS, NZ - 1)), dma((CHUNKS, NZ - 1)),
+            dma((CHUNKS, NX - 1)), dma((CHUNKS, NX - 1)),
+            dma((CHUNKS, NZ - 1)), dma((CHUNKS, NZ - 1)),
+            dma((CHUNKS,)), dma((CHUNKS,)),
+            dma, dma,
+            dma((NZ - 1,)), dma((NZ - 1,)),
+            dma((NX - 1,)), dma((NX - 1,)),
+        ],
+        compiler_params=pltpu.CompilerParams(
+            collective_id=0, has_side_effects=True, vmem_limit_bytes=48 << 20
+        ),
+        name="scan_states",
+    )(states, decay)
+
+
+ROWS = 96
+OWNERS = (NX, NZ, 2)
+
+
+def reduce_kernel(g, out, c_rec, h1, a0, a1, a1r, a2, a2r, b0, b1, b1r, b2, b2r, c0, c1, c1r, c2, c2r, *sems):
+    here = place()
+    x, z, h, yl, core = (here[a] for a in AXES)
+    y = h * 2 + yl
+    cpeer = shifted(here, core=1)
+    lpeer = shifted(here, yl=1)
+    zpeers = [shifted(here, z=d) for d in range(1, NZ)]
+    xpeers = [shifted(here, x=d) for d in range(1, NX)]
+    ynext = [lax.rem(y + d, 4) for d in range(1, 4)]
+    ypeers = [(x, z, t // 2, lax.rem(t, 2), core) for t in ynext]
+    greet([cpeer] + zpeers + xpeers + ypeers)
+    cs, cr, x0s, x0r, y0s, y0r, z0s, z0r, y1s, y1r, z1s, z1r, x1s, x1r, z2s, z2r, x2s, x2r, y2s, y2r, ls, lr, ks, kr = sems
+    keep = pl.multiple_of(core * 48, 8)
+    give = pl.multiple_of((1 - core) * 48, 8)
+    swap = push(g.at[:, :, :, pl.ds(give, 48)], c_rec, cs, cr, cpeer)
+    swap.start()
+    swap.wait()
+    h1[...] = g[:, :, :, pl.ds(keep, 48), :] + c_rec[...]
+
+    def rows(start, there):
+        return pl.ds(pl.multiple_of(start + 8 * lax.rem(there, 2), 8), 8)
+
+    def start(copies):
+        for copy in copies:
+            copy.start()
+        return copies
+
+    def arrived(copies):
+        for copy in copies:
+            copy.wait_recv()
+
+    zs = [lax.rem(z + d, NZ) for d in range(1, NZ)]
+    xs = [lax.rem(x + d, NX) for d in range(1, NX)]
+    z_one = start([push(h1.at[:, t, :, pl.ds(32, 16)], c0.at[z], z0s.at[d], z0r.at[d], zpeers[d]) for d, t in enumerate(zs)])
+    x_one = start([push(h1.at[t, :, :, pl.ds(0, 16)], a0.at[x], x0s.at[d], x0r.at[d], xpeers[d]) for d, t in enumerate(xs)])
+    y_one = start([push(h1.at[:, :, t // 2, rows(16, t)], b0.at[y], y0s.at[d], y0r.at[d], ypeers[d]) for d, t in enumerate(ynext)])
+    arrived(x_one)
+    total = h1[x, :, :, pl.ds(0, 16), :]
+    for t in xs:
+        total = total + a0[t]
+    a1[...] = total
+    y_two = start([push(a1.at[:, t // 2, rows(0, t)], a1r.at[y], y1s.at[d], y1r.at[d], ypeers[d]) for d, t in enumerate(ynext)])
+    arrived(y_one)
+    total = h1[:, :, h, rows(16, yl), :]
+    for t in ynext:
+        total = total + b0[t]
+    b1[...] = total
+    z_two = start([push(b1.at[:, t], b1r.at[z], z1s.at[d], z1r.at[d], zpeers[d]) for d, t in enumerate(zs)])
+    arrived(z_one)
+    total = h1[:, z, :, pl.ds(32, 16), :]
+    for t in zs:
+        total = total + c0[t]
+    c1[...] = total
+    x_two = start([push(c1.at[t], c1r.at[x], x1s.at[d], x1r.at[d], xpeers[d]) for d, t in enumerate(xs)])
+    arrived(y_two)
+    total = a1[:, h, rows(0, yl), :]
+    for t in ynext:
+        total = total + a1r[t]
+    a2[...] = total
+    z_three = start([push(a2.at[t], a2r.at[z], z2s.at[d], z2r.at[d], zpeers[d]) for d, t in enumerate(zs)])
+    arrived(z_two)
+    total = b1[:, z]
+    for t in zs:
+        total = total + b1r[t]
+    b2[...] = total
+    x_three = start([push(b2.at[t], b2r.at[x], x2s.at[d], x2r.at[d], xpeers[d]) for d, t in enumerate(xs)])
+    arrived(x_two)
+    total = c1[x]
+    for t in xs:
+        total = total + c1r[t]
+    c2[...] = total
+    y_three = start([push(c2.at[t // 2, rows(0, t)], c2r.at[y], y2s.at[d], y2r.at[d], ypeers[d]) for d, t in enumerate(ynext)])
+    arrived(z_three)
+    total = a2[z]
+    for t in zs:
+        total = total + a2r[t]
+    out[core, 0, yl] = total
+    arrived(x_three)
+    total = b2[x]
+    for t in xs:
+        total = total + b2r[t]
+    out[core, 1, yl] = total
+    arrived(y_three)
+    total = c2[h, rows(0, yl), :]
+    for t in ynext:
+        total = total + c2r[t]
+    out[core, 2, yl] = total
+    last = push(out.at[core, :, yl], out.at[core, :, yl], ls, lr, lpeer)
+    last.start()
+    last.wait()
+    both = push(out.at[core], out.at[core], ks, kr, cpeer)
+    both.start()
+    both.wait()
+    for copy in x_one + y_one + z_one + x_two + y_two + z_two + x_three + y_three + z_three:
+        copy.wait_send()
+
+
+def reduce_grads(blocks):
+    vmem = pl.BlockSpec(memory_space=pltpu.VMEM)
+    dma = pltpu.SemaphoreType.DMA
+
+    def f32(*shape):
+        return pltpu.VMEM(shape + (128,), jnp.float32)
+
+    pairs = []
+    for n in (1, 3, 3, 7, 3, 7, 3, 7, 3, 3, 1, 1):
+        pairs += [dma if n == 1 else dma((n,))] * 2
+    return pl.pallas_call(
+        reduce_kernel,
+        out_shape=jax.ShapeDtypeStruct((2, 3, 2, 8, 128), jnp.float32),
+        in_specs=[vmem],
+        out_specs=vmem,
+        scratch_shapes=[
+            f32(4, 8, 2, 48), f32(4, 8, 2, 48),
+            f32(4, 8, 2, 16), f32(8, 2, 16), f32(4, 8, 8), f32(8, 8), f32(8, 8),
+            f32(4, 4, 8, 8), f32(4, 8, 8), f32(8, 4, 8), f32(4, 8), f32(4, 8),
+            f32(8, 4, 2, 16), f32(4, 2, 16), f32(4, 2, 16), f32(2, 16), f32(4, 8),
+        ] + pairs,
+        compiler_params=pltpu.CompilerParams(
+            collective_id=1, has_side_effects=True, vmem_limit_bytes=48 << 20
+        ),
+        name="reduce_grads",
+    )(blocks)
 
 
 def body(layer_input, ssm_input, out_grad, b_weight, c_weight, dt_weight, dt_bias, a_log, d_skip):
@@ -66,12 +433,10 @@
     scaled_cotangent = from_start[:, :, None] * cotangent
     local_state = jnp.einsum("shp,sn->hpn", scaled_inputs, proj_b, precision=EXACT)
     local_back = jnp.einsum("thp,tn->hpn", scaled_cotangent, proj_c, precision=EXACT)
-    identity = (
-        jnp.zeros((head_count,), jnp.float32),
-        jnp.zeros((head_count, head_width, state_size), jnp.float32),
-    )
-    carry_in = entering((block_decay, local_state), SEQ, forward_combine, identity, False)[1]
-    carry_out = entering((block_decay, local_back), SEQ, reverse_combine, identity, True)[1]
+    decay = jnp.pad(jnp.exp(block_decay).reshape(2, HALF), ((0, 0), (0, 4)), constant_values=1.0)
+    decay = jnp.broadcast_to(decay[:, :, None], (2, 24, STATE))
+    carries = scan_states(jnp.stack([local_state, local_back]), decay)
+    carry_in, carry_out = carries[0], carries[1]
     spread = cumulative.T[:, :, None] - cumulative.T[:, None, :]
     decay_table = jnp.exp(jnp.where(causal[None], spread, -1e30))
     scores = jnp.dot(proj_c, proj_b.T, precision=EXACT)
@@ -106,25 +471,30 @@
     weights_wide = jnp.concatenate([b_weight, c_weight, dt_weight], axis=1).astype(jnp.float32)
     grad_u = jnp.dot(grad_cols, weights_wide.T, precision=EXACT).astype(jnp.bfloat16)
     u_wide = layer_input.astype(jnp.float32)
-    row_count = layer_input.shape[1] // lax.axis_size(SEQ)
     full_grads = jnp.einsum("td,tk->dk", u_wide, grad_cols, precision=EXACT)
-    summed, small_grads = lax.psum((full_grads, extras), SEQ_DP)
-    row_grads = lax.dynamic_slice_in_dim(summed, lax.axis_index(SEQ) * row_count, row_count, 0)
+    gb = full_grads[:, :128].reshape(64, 40, 128)
+    gc = full_grads[:, 128:256].reshape(64, 40, 128)
+    gd = jnp.pad(full_grads[:, 256:].reshape(64, 40, 40), ((0, 0), (0, 8), (0, 0))).reshape(64, 3, 16, 40)
+    gd = gd.at[:, 2, 8:11].set(extras[None])
+    gd = jnp.pad(jnp.swapaxes(gd, 1, 2).reshape(64, 16, 120), ((0, 0), (0, 0), (0, 8)))
+    blocks = jnp.concatenate([gb, gc, gd], axis=1).reshape(OWNERS + (ROWS, 128))
+    summed = reduce_grads(blocks).reshape(ROWS, 128)
+    packed = summed[80:, :120].reshape(16, 3, 40).swapaxes(0, 1).reshape(48, 40)
     grad_x_out = grad_x.reshape(length, head_count * head_width).astype(jnp.bfloat16)
     return (
         grad_x_out,
         grad_u,
-        row_grads[:, :state_size],
-        row_grads[:, state_size : 2 * state_size],
-        row_grads[:, 2 * state_size :],
-        small_grads[0],
-        small_grads[1],
-        small_grads[2],
+        summed[:40],
+        summed[40:80],
+        packed[:40],
+        packed[40],
+        packed[41],
+        packed[42],
     )
 
 
 def solution(mesh):
-    split = Mesh(mesh.devices.reshape(4, 8, 2, mesh.shape["dp"]), ("seq_0", "seq_1", "seq_2", "dp"))
+    split = Mesh(mesh.devices.reshape(4, 8, 2, 2, 2), AXES)
     placed = (P(DP_SEQ, None), P(DP_SEQ, None), P(DP_SEQ, None), P(), P(), P(), P(), P(), P())
     return jax.shard_map(
         body,

time: 779 us -> 179 us (0.23)
  waiting for transfers between devices: 563 us -> 0 us
  Pallas kernels: 0 us -> 123 us
  blocking collectives: 109 us -> 0 us
  other arithmetic: 40.2 us -> 6.81 us
  between operations: 15.2 us -> 1.15 us
  matrix products: 40.1 us -> 28.2 us
  local copies, waits for them, and re-layouts: 10.2 us -> 19.4 us
    all_gather x6 -> x0, waiting for transfers between devices: 383 us -> none  [entering(): pieces = jax.tree.map(lambda part: lax.all_gather(part, axis), running)]
    psum x1 -> x0, waiting for transfers between devices: 180 us -> none  [body(): summed, small_grads = lax.psum((full_grads, extras), SEQ_DP)]
    pallas_call x0 -> x2, Pallas kernels: none -> 123 us  [the longest x1 83.3 us: scan_states(): pl.pallas_call(scan_kernel, out_shape=jax.ShapeDtypeStruct(states.shape,...]
    psum x1 -> x0, blocking collectives: 77.2 us -> none  [body(): summed, small_grads = lax.psum((full_grads, extras), SEQ_DP)]
    all_gather x4 -> x0, blocking collectives: 31.6 us -> none  [entering(): pieces = jax.tree.map(lambda part: lax.all_gather(part, axis), running)]
    add x4 -> x1, other arithmetic: 17.9 us -> 0.19 us  [body(): cross_term + jnp.sum(own_out, axis=0)]
    reduce_sum x1, other arithmetic: 13 us -> 0.39 us  [body(): jnp.sum(carry_out * carry_in, axis=(1, 2))]
  transfers between devices with their start and end apart: 7 -> 0, of which waited for: 7 -> 0; matrix products, arithmetic and copies ran while one was open for 5% -> 0% of each run, Pallas kernels for 0% -> 0%
where the time goes in v1:
time: 179 us; the launch traced here: 178 us
  Pallas kernels  123 us (69%)
  matrix products  28.2 us (16%)
  local copies, waits for them, and re-layouts  19.4 us (11%)
  other arithmetic  6.81 us (4%)
    pallas_call x1, Pallas kernels, scan_states(): pl.pallas_call(scan_kernel, out_shape=jax.ShapeDtypeStruct(states.shape,...  83.3 us
    pallas_call x1, Pallas kernels, reduce_grads(): pl.pallas_call(reduce_kernel, out_shape=jax.ShapeDtypeStruct((2, 3, 2, 8,...  39.4 us
    unnamed x62, local copies, waits for them, and re-layouts  7.84 us
    slice x2, local copies, waits for them, and re-layouts, body(): gb = full_grads[:, :128].reshape(64, 40, 128)  4.23 us
    dot_general x1, matrix products, body(): back_in = jnp.einsum('hst,shp->thp', weight, cotangent, precision=EXACT)  3.86 us

profile of v1, /device:TPU:1, one launch (start us, length us, event | category | flops | bytes accessed | tf_op | source)
XLA Modules:
  0.0 178.2 jit_solution(17362501203792689475)
XLA Ops:
  0.7 0.8 exponential_negate_fusion
  2.0 1.9 %compare_select_fusion = (f32[40,128]{1,0:T(8,128)}, f32[128,40]{0,1:T(8,128)S(1)}) fusion(f32[40]{0:T(128)} %param.17, bf16[128,2560]{1,0:T(8,128)(2,1)S(1)} %copy-done, bf16[2560,40]{0,1:T(8,128)(2,1)} %param.16), kind=kOutput, calls=%fused_computation.61 | convolution fusion | flops 26250240 | bytes 901280 | tf_op jit(solution)/shard_map/dot_general | solution.py:418
  4.5 1.5 fusion.80
  6.3 0.9 fusion.81
  7.2 0.7 fusion.73
  8.8 1.1 copy.67
  9.9 1.2 convolution_bitcast_fusion.1
  11.1 1.2 convolution_bitcast_fusion.2
  12.6 83.3 %scan_states.1 = f32[2,40,64,128]{3,2,1,0:T(8,128)S(1)} custom-call(f32[2,40,64,128]{3,2,1,0:T(8,128)S(1)} %pad_maximum_fusion.1.sr, f32[2,24,128]{2,1,0:T(8,128)S(1)} %broadcast_in_dim.12.dec), custom_call_target="tpu_custom_call" | custom-call | tf_op jit(solution)/shard_map/scan_states/pallas_call | solution.py:247
  96.4 2.9 %fusion.31 = f32[128,40]{0,1:T(8,128)} fusion(f32[2,40,64,128]{3,2,1,0:T(8,128)S(1)} %scan_states.1, f32[128,128]{1,0:T(8,128)S(1)} %fusion.79, bf16[128,40,64]{0,2,1:T(8,128)(2,1)} %bitcast.129), kind=kOutput, calls=%fused_computation.43 | convolution fusion | flops 504294400 | bytes 2052096 | tf_op jit(solution)/shard_map/hpn,tn->thp/dot_general | solution.py:456
  99.3 1.2 fusion.22
  100.6 3.9 %multiply_reduce_fusion.2 = (f32[128,40]{0,1:T(8,128)}, f32[128,40]{0,1:T(8,128)}, bf16[128,40,64]{0,2,1:T(8,128)(2,1)}) fusion(f32[128,40,64]{0,2,1:T(8,128)S(1)} %fusion.22, f32[40]{0:T(128)S(1)} %copy-done.22, f32[128,40]{0,1:T(8,128)S(1)} %get-tuple-element.74, f32[128,40]{0,1:T(8,128)S(1)} %copy-done.21, bf16[128,40,64]{0,2,1:T(8,128)(2,1)S(1)} %bitcast.131, ...), kind=kOutput, calls=%fused_computation.33 | convolution fusion | flops 509204480 | bytes 3461280 | tf_op jit(solution)/shard_map/hst,shp->thp/dot_general | solution.py:445
  104.4 2.2 %copy.74 = bf16[128,2560]{1,0:T(8,128)(2,1)} copy(bf16[128,2560]{0,1:T(8,128)(2,1)} %bitcast.143) | data formatting | bytes 1310720
  107.1 3.3 %fusion.8 = (f32[40,128]{1,0:T(8,128)S(1)}, f32[40,128]{1,0:T(8,128)S(1)}, f32[40,128,128]{2,1,0:T(8,128)S(1)}) fusion(f32[40,128]{1,0:T(8,128)} %get-tuple-element.76, f32[128,128]{1,0:T(8,128)} %fusion.81, f32[40,128]{1,0:T(8,128)S(1)} %bitcast.145, pred[128,128]{1,0:T(8,128)(4,1)} %copy-done.15, bf16[128,40,64]{0,2,1:T(8,128)(2,1)} %bitcast.130, ...), kind=kOutput, calls=%fused_computation.14 | convolution fusion | flops 88463360 | bytes 4096000 | tf_op jit(solution)/shard_map/thp,shp->hts/dot_general | solution.py:443
  110.9 1.2 multiply_reduce_fusion
  112.6 2.2 %fusion.38 = f32[128,128]{0,1:T(8,128)S(1)} fusion(f32[128,40,64]{0,2,1:T(8,128)S(1)} %bitcast.136, f32[2,40,64,128]{3,2,1,0:T(8,128)S(1)} %scan_states.1), kind=kOutput, calls=%fused_computation.50 | convolution fusion | flops 503316480 | bytes 2686976 | tf_op jit(solution)/shard_map/thp,hpn->tn/dot_general | solution.py:452
  114.9 2.3 %fusion.41 = f32[128,128]{0,1:T(8,128)S(1)} fusion(f32[128,40,64]{0,2,1:T(8,128)S(1)} %bitcast.135, f32[2,40,64,128]{3,2,1,0:T(8,128)S(1)} %scan_states.1), kind=kOutput, calls=%fused_computation.51 | convolution fusion | flops 503316480 | bytes 2686976 | tf_op jit(solution)/shard_map/thp,hpn->tn/dot_general | solution.py:454
  117.7 3.0 %convolution_convert_fusion = bf16[128,2560]{1,0:T(8,128)(2,1)} fusion(bf16[2560,40]{1,0:T(8,128)(2,1)S(1)} %copy-done.14, bf16[2560,128]{1,0:T(8,128)(2,1)S(1)} %copy-done.12, bf16[2560,128]{1,0:T(8,128)(2,1)S(1)} %copy-done.13, f32[128,40]{0,1:T(8,128)S(1)} %get-tuple-element.59, f32[128,128]{0,1:T(8,128)S(1)} %convolution_add_fusion, ...), kind=kOutput, calls=%fused_computation.1 | convolution fusion | flops 1168869376 | bytes 2322432 | tf_op jit(solution)/shard_map/dot_general | solution.py:472
  120.9 1.3 convolution_bitcast_fusion
  122.3 1.4 fusion.75
  123.7 0.6 copy-done.1
  124.3 2.8 %copy.68 = f32[2560,128]{1,0:T(8,128)} copy(f32[2560,128]{0,1:T(8,128)} %get-tuple-element.62) | data formatting | bytes 2621440 | tf_op jit(solution)/shard_map/slice | solution.py:475
  127.1 2.1 %reshape.134 = f32[64,40,40]{1,0,2:T(8,128)} reshape(f32[2560,40]{0,1:T(8,128)S(1)} %slice-done) | data formatting | bytes 819200 | tf_op jit(solution)/shard_map/reshape | solution.py:477
  129.3 1.7 copy.86
  131.2 1.1 copy.87
  132.4 1.1 pad.18.clone
  133.4 1.5 copy.69
  134.9 2.1 %pad_maximum_fusion.g = f32[4,8,2,96,128]{4,3,2,1,0:T(8,128)S(1)} fusion(f32[4,8,2,16,128]{4,3,2,1,0:T(8,128)S(1)} %bitcast.142, f32[4,8,2,40,128]{4,3,2,1,0:T(8,128)} %bitcast.138, f32[4,8,2,40,128]{4,3,2,1,0:T(8,128)} %bitcast.137), kind=kLoop, calls=%fused_computation.2 | loop fusion | flops 1572864 | bytes 6291456 | tf_op jit(solution)/shard_map/concatenate | solution.py:480
  137.0 39.4 %reduce_grads.1 = f32[2,3,2,8,128]{4,3,2,1,0:T(8,128)S(1)} custom-call(f32[4,8,2,96,128]{4,3,2,1,0:T(8,128)S(1)} %pad_maximum_fusion.g), custom_call_target="tpu_custom_call" | custom-call | tf_op jit(solution)/shard_map/reduce_grads/pallas_call | solution.py:393
  176.4 0.6 fusion.76
  177.1 0.5 slice_bitcast_fusion
  177.6 0.6 slice.90
  (87 shorter events, 5.5 us)
Async XLA Ops:
  0.6 1.3 copy-start
  0.6 5.3 %copy-start.11 = (bf16[2560,128]{1,0:T(8,128)(2,1)S(1)}, bf16[2560,128]{1,0:T(8,128)(2,1)}, u32[]{:S(2)}) copy-start(bf16[2560,128]{1,0:T(8,128)(2,1)} %param.15) | copy-start | bytes 1966084
  1.4 2.7 %copy-start.24 = (f32[40]{0:T(128)}, f32[40]{0:T(128)S(1)}, u32[]{:S(2)}) copy-start(f32[40]{0:T(128)S(1)} %exponential_negate_fusion) | copy-start | bytes 484
  2.0 98.6 %copy-start.15 = (pred[128,128]{1,0:T(8,128)(4,1)}, pred[128,128]{1,0:T(8,128)(4,1)S(1)}, u32[]{:S(2)}) copy-start(pred[128,128]{1,0:T(8,128)(4,1)S(1)} %iota_compare_fusion) | copy-start | bytes 49156
  4.5 3.4 %copy-start.9 = (bf16[128,2560]{1,0:T(8,128)(2,1)S(1)}, bf16[128,2560]{1,0:T(8,128)(2,1)}, u32[]{:S(2)}) copy-start(bf16[128,2560]{1,0:T(8,128)(2,1)} %param.12) | copy-start | bytes 1966084
  6.0 2.3 %copy-start.10 = (bf16[128,2560]{1,0:T(8,128)(2,1)S(1)}, bf16[128,2560]{1,0:T(8,128)(2,1)}, u32[]{:S(2)}) copy-start(bf16[128,2560]{1,0:T(8,128)(2,1)} %param.13) | copy-start | bytes 1966084
  7.9 0.9 copy-start.8
  8.2 2.9 %copy-start.5 = (bf16[128,2560]{0,1:T(8,128)(2,1)}, bf16[128,2560]{0,1:T(8,128)(2,1)S(1)}, u32[]{:S(2)}) copy-start(bf16[128,2560]{0,1:T(8,128)(2,1)S(1)} %copy.62) | copy-start | bytes 1966084
  8.6 2.5 %copy-start.2 = (bf16[128,2560]{0,1:T(8,128)(2,1)}, bf16[128,2560]{0,1:T(8,128)(2,1)S(1)}, u32[]{:S(2)}) copy-start(bf16[128,2560]{0,1:T(8,128)(2,1)S(1)} %copy.61) | copy-start | bytes 1966084
  99.3 1.3 copy-start.3
  99.3 1.3 copy-start.6
  99.3 1.3 copy-start.17
  99.3 1.3 copy-start.21
  99.3 1.3 copy-start.22
  104.4 2.2 %copy-start.19 = (f32[128,40]{0,1:T(8,128)S(1)}, f32[128,40]{0,1:T(8,128)}, u32[]{:S(2)}) copy-start(f32[128,40]{0,1:T(8,128)} %get-tuple-element.54) | copy-start | bytes 61444
  107.0 3.4 %copy-start.18 = (f32[128,40]{0,1:T(8,128)S(1)}, f32[128,40]{0,1:T(8,128)}, u32[]{:S(2)}) copy-start(f32[128,40]{0,1:T(8,128)} %fusion.31) | copy-start | bytes 61444
  107.0 3.4 %copy-start.20 = (f32[128,40]{0,1:T(8,128)S(1)}, f32[128,40]{0,1:T(8,128)}, u32[]{:S(2)}) copy-start(f32[128,40]{0,1:T(8,128)} %get-tuple-element.54) | copy-start | bytes 61444
  107.0 3.4 %copy-start.25 = (f32[40]{0:T(128)S(1)}, f32[40]{0:T(128)}, u32[]{:S(2)}) copy-start(f32[40]{0:T(128)} %copy-done.24) | copy-start | bytes 484
  107.1 3.4 %copy-start.26 = (f32[128]{0:T(128)S(1)}, f32[128]{0:T(128)}, u32[]{:S(2)}) copy-start(f32[128]{0:T(128)} %compare_convert_fusion) | copy-start | bytes 1540
  107.1 3.4 %copy-start.27 = (f32[128,40]{0,1:T(8,128)S(1)}, f32[128,40]{0,1:T(8,128)}, u32[]{:S(2)}) copy-start(f32[128,40]{0,1:T(8,128)} %get-tuple-element.55) | copy-start | bytes 61444
  107.1 3.8 %copy-start.23 = (f32[40]{0:T(128)S(1)}, f32[40]{0:T(128)}, u32[]{:S(2)}) copy-start(f32[40]{0:T(128)} %param.18) | copy-start | bytes 484
  107.1 3.8 %copy-start.16 = (pred[128,128]{1,0:T(8,128)(4,1)S(1)}, pred[128,128]{1,0:T(8,128)(4,1)}, u32[]{:S(2)}) copy-start(pred[128,128]{1,0:T(8,128)(4,1)} %copy-done.15) | copy-start | bytes 49156
  110.9 1.2 copy-start.4
  110.9 1.3 copy-start.7
  114.8 2.9 %copy-start.12 = (bf16[2560,128]{1,0:T(8,128)(2,1)S(1)}, bf16[2560,128]{1,0:T(8,128)(2,1)}, u32[]{:S(2)}) copy-start(bf16[2560,128]{1,0:T(8,128)(2,1)} %param.15) | copy-start | bytes 1966084
  114.9 2.9 %copy-start.13 = (bf16[2560,128]{1,0:T(8,128)(2,1)S(1)}, bf16[2560,128]{1,0:T(8,128)(2,1)}, u32[]{:S(2)}) copy-start(bf16[2560,128]{1,0:T(8,128)(2,1)} %param.14) | copy-start | bytes 1966084
  114.9 2.9 %copy-start.14 = (bf16[2560,40]{1,0:T(8,128)(2,1)S(1)}, bf16[2560,40]{1,0:T(8,128)(2,1)}, u32[]{:S(2)}) copy-start(bf16[2560,40]{1,0:T(8,128)(2,1)} %copy.67) | copy-start | bytes 614404
  122.3 2.0 %copy-start.1 = (f32[2560,296]{0,1:T(8,128)}, f32[2560,296]{0,1:T(8,128)S(1)}, u32[]{:S(2)}) copy-start(f32[2560,296]{0,1:T(8,128)S(1)} %convolution_bitcast_fusion) | copy-start | bytes 9093124
  124.3 2.8 %slice-start = ((f32[2560,296]{0,1:T(8,128)}), f32[2560,40]{0,1:T(8,128)S(1)}, s32[]{:S(2)}) async-start(f32[2560,296]{0,1:T(8,128)} %copy-done.1), calls=%async_computation | async-start | bytes 819200 | tf_op jit(solution)/shard_map/slice | solution.py:477

commit v2 on v1

v2 whole, which is shorter than its diff:
```python
import jax
import jax.numpy as jnp
from jax import lax
from jax.experimental import pallas as pl
from jax.experimental.pallas import tpu as pltpu
from jax.sharding import Mesh
from jax.sharding import PartitionSpec as P

SEQ = ("x", "z", "yh")
DP_SEQ = ("yl", "core", "x", "z", "yh")
AXES = ("x", "z", "yh", "yl", "core")
SIZES = {"x": 4, "z": 8, "yh": 2, "yl": 2, "core": 2}
MESH = pl.DeviceIdType.MESH
HEADS, WIDTH, STATE = 40, 64, 128
HALF = HEADS // 2
CHUNK = 4
CHUNKS = HALF // CHUNK
NX, NZ = SIZES["x"], SIZES["z"]
PIECE = WIDTH // NZ


def place():
    return {axis: lax.axis_index(axis) for axis in AXES}


def shifted(here, **steps):
    there = dict(here)
    for axis, step in steps.items():
        there[axis] = lax.rem(here[axis] + step, SIZES[axis])
    return tuple(there[axis] for axis in AXES)


def greet(peers):
    barrier = pltpu.get_barrier_semaphore()
    for peer in peers:
        pl.semaphore_signal(barrier, inc=1, device_id=peer, device_id_type=MESH)
    pl.semaphore_wait(barrier, len(peers))


def push(src, dst, send, recv, peer):
    return pltpu.make_async_remote_copy(
        src_ref=src, dst_ref=dst, send_sem=send, recv_sem=recv, device_id=peer, device_id_type=MESH
    )


TOK = 128
MODEL = 2560
ROWS = 96
BLOCK = CHUNK * WIDTH
F32, BF16 = jnp.float32, jnp.bfloat16


def dot(a, b):
    return jnp.dot(a, b, preferred_element_type=F32)


def dot_tn(a, b):
    return lax.dot_general(a, b, (((0,), (0,)), ((), ())), preferred_element_type=F32)


def dot_nt(a, b):
    return lax.dot_general(a, b, (((1,), (1,)), ((), ())), preferred_element_type=F32)


def split(v):
    top = v.astype(BF16)
    return top, (v - top.astype(F32)).astype(BF16)


def wide(v):
    return jnp.concatenate(split(v), axis=1)


def tall(v):
    return jnp.concatenate(split(v), axis=0)


def square(v):
    w = wide(v)
    return jnp.concatenate([w, w], axis=0)


def fold(p):
    return p[:, :128] + p[:, 128:]


def padded(v):
    return jnp.concatenate([v, jnp.zeros((TOK - v.shape[0], TOK), F32)], axis=0)


def layer_kernel(
    u_ref, x_ref, g_ref, wb_ref, wc_ref, wd_ref, bias_ref, alog_ref, skip_ref,
    gx_ref, gu_ref, gbw_ref, gcw_ref, gdw_ref, ex_ref,
    xt, gt, ut, xw, gw, b4, c4, bt4, ct4, scores, pairacc, rowacc, inner, gbacc, gcacc,
    rows_dt, rows_ws, rows_fs, rows_te, rows_cum, rows_skip, rows_col, rows_xb, rows_gf, rows_cross, rows_gx,
    flat_dt, flat_raw, gwd, sr, dec, car, par, pq, arec, xs, xr, bs, ps, ys, dpar, coef, pair, zd, rd,
    grad, c_rec, h1, a0, a1, a1r, a2, a2r, b0, b1, b1r, b2, b2r, c0, c1, c1r, c2, c2r, fin,
    *sems,
):
    here = place()
    x, z, h, yl, core = (here[a] for a in AXES)
    y = h * 2 + yl
    low = h == 0
    mine, other = h * HALF, (1 - h) * HALF
    partner = shifted(here, yh=1)
    cpeer = shifted(here, core=1)
    lpeer = shifted(here, yl=1)
    zpeers = [shifted(here, z=d) for d in range(1, NZ)]
    xpeers = [shifted(here, x=d) for d in range(1, NX)]
    ynext = [lax.rem(y + d, 4) for d in range(1, 4)]
    ypeers = [(x, z, t // 2, lax.rem(t, 2), core) for t in ynext]
    peers = [cpeer] + ypeers + zpeers + xpeers
    scan_sems, red_sems = sems[:16], sems[16:]
    y1s, y1r, as_, ar_, xss, xrs, bss, brs, y2s, y2r, d1s, d1r, d2s, d2r, d3s, d3r = scan_sems
    barrier = pltpu.get_barrier_semaphore()
    for peer in peers:
        pl.semaphore_signal(barrier, inc=1, device_id=peer, device_id_type=MESH)

    u = u_ref[...]
    raw = dot(u, wd_ref[...])
    raw = jnp.concatenate([raw, jnp.zeros((TOK, TOK - HEADS), F32)], axis=1)
    raw = raw.T[:HEADS] + bias_ref[...]
    small = jnp.exp(-jnp.abs(raw))
    above = 1.0 + small
    gap = above - 1.0
    log_part = jnp.where(gap == 0.0, small, jnp.log(above) * (small / jnp.where(gap == 0.0, 1.0, gap)))
    dt = jnp.maximum(raw, 0.0) + log_part
    rate = -jnp.exp(alog_ref[...])
    row_i = lax.broadcasted_iota(jnp.int32, (TOK, TOK), 0)
    col_i = lax.broadcasted_iota(jnp.int32, (TOK, TOK), 1)
    upto = (row_i <= col_i).astype(F32)
    since = (row_i >= col_i).astype(F32)
    cum = jnp.dot(dt * rate, upto, precision=lax.Precision.HIGHEST, preferred_element_type=F32)
    last = cum[:, TOK - 1 :]
    to_end = jnp.exp(last - cum)
    from_start = jnp.exp(cum)
    flat_dt[...] = dt
    flat_raw[...] = raw

    def rows(v):
        return v.reshape(HEADS, 1, TOK)

    rows_dt[...] = rows(dt)
    rows_ws[...] = rows(to_end * dt)
    rows_fs[...] = rows(from_start)
    rows_te[...] = rows(to_end)
    rows_cum[...] = rows(cum)
    rows_skip[...] = rows(jnp.broadcast_to(skip_ref[...], (HEADS, TOK)))
    decay = jnp.broadcast_to(jnp.exp(last), (HEADS, STATE))
    fill = jnp.ones((4, STATE), F32)
    dec[0] = jnp.concatenate([decay[:HALF], fill], axis=0)
    dec[1] = jnp.concatenate([decay[HALF:], fill], axis=0)
    proj_b = dot(u, wb_ref[...])
    proj_c = dot(u, wc_ref[...])
    b4[...] = square(proj_b)
    c4[...] = square(proj_c)

    def states(first):
        at = pl.multiple_of(first * WIDTH, BLOCK)
        heads = pl.ds(first, CHUNK)
        rows_at = pl.ds(at, BLOCK)
        xc = x_ref[:, pl.ds(at, BLOCK)].T
        gc = g_ref[:, pl.ds(at, BLOCK)].T
        xt[rows_at, :] = xc
        gt[rows_at, :] = gc
        xsc = xc.astype(F32).reshape(CHUNK, WIDTH, TOK) * rows_ws[heads]
        gsc = gc.astype(F32).reshape(CHUNK, WIDTH, TOK) * rows_fs[heads]
        xwc = wide(xsc.reshape(BLOCK, TOK))
        gwc = wide(gsc.reshape(BLOCK, TOK))
        xw[rows_at, :] = xwc
        gw[rows_at, :] = gwc
        sr[0, heads] = fold(dot(xwc, b4[...])).reshape(CHUNK, WIDTH, STATE)
        sr[1, heads] = fold(dot(gwc, c4[...])).reshape(CHUNK, WIDTH, STATE)

    states(other)
    pl.semaphore_wait(barrier, len(peers))
    first = push(dec.at[1 - h], dpar, d1s, d1r, partner)
    first.start()
    y1 = [
        push(
            sr.at[:, pl.ds(other + c * CHUNK, CHUNK)],
            par.at[:, pl.ds(c * CHUNK, CHUNK)],
            y1s.at[c], y1r.at[c], partner,
        )
        for c in range(CHUNKS)
    ]
    y1[0].start()
    states(other + CHUNK)
    y1[1].start()
    xr[x] = jnp.zeros((HALF, PIECE, STATE), F32)
    first.wait()
    own_decay = dec[h]
    par_decay = dpar[...]
    one = jnp.ones_like(own_decay)
    coef[0] = jnp.where(low, par_decay, one)
    coef[1] = jnp.where(low, one, own_decay)
    coef[2] = jnp.where(low, one, par_decay)
    coef[3] = jnp.where(low, own_decay, one)
    pair[...] = own_decay * par_decay
    zd[z] = own_decay * par_decay
    second = [push(pair, zd.at[z], d2s.at[d], d2r.at[d], peer) for d, peer in enumerate(zpeers)]
    for copy in second:
        copy.start()
    states(mine)
    for c in range(2, CHUNKS):
        states(other + c * CHUNK)
    bt4[...] = square(proj_b.T)
    ct4[...] = square(proj_c.T)
    scores[...] = jnp.where(row_i >= col_i, fold(dot(wide(proj_c), bt4[...])), 0.0)
    pairacc[...] = jnp.zeros((TOK, TOK), F32)
    rowacc[...] = jnp.zeros((TOK, TOK), F32)
    for copy in second:
        copy.wait()
    row = zd[0]
    for k in range(1, NZ):
        row = row * zd[k]
    rd[x] = row
    third = [push(rd.at[x], rd.at[x], d3s.at[d], d3r.at[d], peer) for d, peer in enumerate(xpeers)]
    for copy in third:
        copy.start()

    def a_copies(c):
        heads = pl.ds(c * CHUNK, CHUNK)
        copies = []
        for d, peer in enumerate(zpeers):
            pz = pl.multiple_of(lax.rem(z + d + 1, NZ) * PIECE, PIECE)
            copies.append(
                push(pq.at[:, heads, pl.ds(pz, PIECE)], arec.at[z, :, heads], as_.at[c, d], ar_.at[c, d], peer)
            )
        return copies

    def x_copies(c):
        heads = pl.ds(c * CHUNK, CHUNK)
        copies = []
        for d, peer in enumerate(xpeers):
            px = lax.rem(x + d + 1, NX)
            back = jnp.where(px > x, 0, 1)
            copies.append(push(xs.at[back, heads], xr.at[x, heads], xss.at[c, d], xrs.at[c, d], peer))
        return copies

    def b_copies(c):
        heads = pl.ds(c * CHUNK, CHUNK)
        here_rows = pl.ds(pl.multiple_of(z * PIECE, PIECE), PIECE)
        copies = []
        for d, peer in enumerate(zpeers):
            pz = lax.rem(z + d + 1, NZ)
            copies.append(
                push(bs.at[pz, :, heads], ps.at[:, heads, here_rows], bss.at[c, d], brs.at[c, d], peer)
            )
        return copies

    def y2_copy(c):
        return push(
            ys.at[:, pl.ds(c * CHUNK, CHUNK)],
            car.at[:, pl.ds(mine + c * CHUNK, CHUNK)],
            y2s.at[c], y2r.at[c], partner,
        )

    def pairs(c):
        y1[c].wait_recv()
        if c + 2 < CHUNKS:
            y1[c + 2].start()

        def head(i, carry):
            k = c * CHUNK + i
            at = pl.ds(k, 1)
            pq[0, k] = coef[0, at, :] * sr[0, mine + k] + coef[1, at, :] * par[0, k]
            pq[1, k] = coef[2, at, :] * sr[1, mine + k] + coef[3, at, :] * par[1, k]
            return carry

        lax.fori_loop(0, CHUNK, head, 0)
        heads = pl.ds(c * CHUNK, CHUNK)
        own = pl.ds(pl.multiple_of(z * PIECE, PIECE), PIECE)
        arec[z, :, heads] = pq[:, heads, own, :]
        for copy in a_copies(c):
            copy.start()

    def totals(c):
        for copy in a_copies(c):
            copy.wait_recv()

        def head(i, carry):
            k = c * CHUNK + i
            at = pl.ds(k, 1)
            forward = arec[0, 0, k]
            backward = arec[NZ - 1, 1, k]
            for j in range(1, NZ):
                forward = zd[j, at, :] * forward + arec[j, 0, k]
                backward = zd[NZ - 1 - j, at, :] * backward + arec[NZ - 1 - j, 1, k]
            xs[0, k] = forward
            xs[1, k] = backward
            return carry

        lax.fori_loop(0, CHUNK, head, 0)
        for copy in x_copies(c):
            copy.start()

    def prefixes(c):
        if c == 0:
            for copy in third:
                copy.wait()
        for copy in x_copies(c):
            copy.wait_recv()

        def head(i, carry):
            k = c * CHUNK + i
            at = pl.ds(k, 1)
            forward = jnp.zeros((PIECE, STATE), jnp.float32)
            backward = jnp.zeros((PIECE, STATE), jnp.float32)
            for j in range(NX):
                forward = jnp.where(j < x, rd[j, at, :] * forward + xr[j, k], forward)
                m = NX - 1 - j
                backward = jnp.where(m > x, rd[m, at, :] * backward + xr[m, k], backward)
            for j in range(NZ):
                bs[j, 0, k] = forward
                forward = zd[j, at, :] * forward + arec[j, 0, k]
                m = NZ - 1 - j
                bs[m, 1, k] = backward
                backward = zd[m, at, :] * backward + arec[m, 1, k]
            return carry

        lax.fori_loop(0, CHUNK, head, 0)
        heads = pl.ds(c * CHUNK, CHUNK)
        own = pl.ds(pl.multiple_of(z * PIECE, PIECE), PIECE)
        ps[:, heads, own, :] = bs[z, :, heads]
        for copy in b_copies(c):
            copy.start()

    def finals(c):
        for copy in b_copies(c):
            copy.wait_recv()

        def head(i, carry):
            k = c * CHUNK + i
            at = pl.ds(k, 1)
            before, after = ps[0, k], ps[1, k]
            zero = jnp.zeros_like(before)
            ys[0, k] = coef[3, at, :] * before + jnp.where(low, sr[0, mine + k], zero)
            ys[1, k] = coef[1, at, :] * after + jnp.where(low, zero, sr[1, mine + k])
            car[0, mine + k] = coef[2, at, :] * before + jnp.where(low, zero, par[0, k])
            car[1, mine + k] = coef[0, at, :] * after + jnp.where(low, par[1, k], zero)
            return carry

        lax.fori_loop(0, CHUNK, head, 0)
        y2_copy(c).start()


    def within(start, count):
        def two(i, carry):
            for j in range(2):
                k = start + 2 * i + j
                at = pl.ds(pl.multiple_of(k * WIDTH, WIDTH), WIDTH)
                gk = gt[at, :]
                dots = dot_tn(gk, xt[at, :])
                across = jnp.broadcast_to(rows_cum[k], (TOK, TOK))
                table = jnp.exp(jnp.minimum(across.T - across, 0.0))
                weight = table * scores[...]
                inner[at, :] = fold(dot(gk, wide(weight)))
                terms = weight * dots
                rows_col[k] = jnp.sum(terms, axis=0, keepdims=True)
                pairacc[...] += table * dots * rows_dt[k]
                sums = jnp.sum(terms * rows_dt[k], axis=1, keepdims=True)
                rowacc[...] = jnp.where(col_i == k, sums, rowacc[...])
            return carry

        lax.fori_loop(0, count // 2, two, 0)

    gbacc[...] = jnp.zeros((2 * TOK, 2 * TOK), F32)
    gcacc[...] = jnp.zeros((2 * TOK, 2 * TOK), F32)

    def outputs(first):
        at = pl.multiple_of(first * WIDTH, BLOCK)
        heads = pl.ds(first, CHUNK)
        rows_at = pl.ds(at, BLOCK)
        ci = car[0, heads]
        co = car[1, heads]
        rows_cross[heads] = jnp.sum(ci * co, axis=1, keepdims=True)
        ciw = wide(ci.reshape(BLOCK, STATE))
        cow = wide(co.reshape(BLOCK, STATE))
        back = fold(dot(cow, bt4[...])).reshape(CHUNK, WIDTH, TOK)
        front = fold(dot(ciw, ct4[...])).reshape(CHUNK, WIDTH, TOK)
        gbacc[...] += dot_tn(xw[rows_at, :], cow)
        gcacc[...] += dot_tn(gw[rows_at, :], ciw)
        xf = xt[rows_at, :].astype(F32).reshape(CHUNK, WIDTH, TOK)
        gf = gt[rows_at, :].astype(F32).reshape(CHUNK, WIDTH, TOK)
        rows_xb[heads] = jnp.sum(xf * back, axis=1, keepdims=True)
        rows_gf[heads] = jnp.sum(gf * front, axis=1, keepdims=True)
        rows_gx[heads] = jnp.sum(gf * xf, axis=1, keepdims=True)
        total = inner[rows_at, :].reshape(CHUNK, WIDTH, TOK) + rows_te[heads] * back
        gx = rows_dt[heads] * total + rows_skip[heads] * gf
        gx_ref[:, pl.ds(at, BLOCK)] = gx.reshape(BLOCK, TOK).T.astype(BF16)

    within(other, 4)
    for c in range(1, CHUNKS):
        states(mine + c * CHUNK)
    within(other + 4, 4)
    for step in range(CHUNKS + 3):
        if step < CHUNKS:
            pairs(step)
        if 0 <= step - 1 < CHUNKS:
            totals(step - 1)
        if 0 <= step - 2 < CHUNKS:
            prefixes(step - 2)
        if 0 <= step - 3 < CHUNKS:
            finals(step - 3)
        if step < 3:
            within(other + 8 + 4 * step, 4)
        else:
            within(mine + 4 * (step - 3), 4)
            outputs(mine + 4 * (step - 3))
        if step == 5:
            for j in range(0, MODEL, 512):
                ut[j : j + 512, :] = u_ref[:, j : j + 512].T
    for c in range(CHUNKS):
        y2_copy(c).wait_recv()
        outputs(other + c * CHUNK)

    sums = pairacc[...]
    sums = jnp.where(row_i >= col_i, sums, 0.0)
    sumw = wide(sums)
    acc = gbacc[...] + dot_tn(sumw, wide(dot(u_ref[...], wc_ref[...])))
    acc = acc[:TOK] + acc[TOK:]
    grad_b = fold(acc)
    acc = gcacc[...]
    acc = acc[:TOK] + acc[TOK:]
    grad_c = fold(acc) + fold(dot(sumw, b4[...]))

    def flat(ref):
        return ref[...].reshape(HEADS, TOK)

    dt = flat_dt[...]
    raw = flat_raw[...]
    end = flat(rows_te)
    rate = -jnp.exp(alog_ref[...])
    col = flat(rows_col)
    xb = end * flat(rows_xb)
    direct = col + xb
    own_out = dt * xb
    own_in = flat(rows_fs) * flat(rows_gf)
    cross = flat(rows_fs)[:, TOK - 1 :] * jnp.sum(flat(rows_cross), axis=1, keepdims=True)
    change = rowacc[...].T[:HEADS] - dt * col + own_in - own_out
    lanes = lax.broadcasted_iota(jnp.int32, (HEADS, TOK), 1)
    edge = cross + jnp.sum(own_out, axis=1, keepdims=True)
    change = change + jnp.where(lanes == TOK - 1, edge, 0.0)
    grad_log = jnp.dot(change, since, precision=lax.Precision.HIGHEST, preferred_element_type=F32)
    grad_raw = (direct + grad_log * rate) * (1.0 / (1.0 + jnp.exp(-raw)))
    grad_bias = jnp.sum(grad_raw, axis=1, keepdims=True)
    grad_alog = jnp.sum(grad_log * dt, axis=1, keepdims=True) * rate
    grad_skip = jnp.sum(flat(rows_gx), axis=1, keepdims=True)
    extra = jnp.where(lanes == 0, grad_bias, jnp.where(lanes == 1, grad_alog, jnp.where(lanes == 2, grad_skip, 0.0)))
    extra = padded(extra).T[:8]
    grad_d = padded(grad_raw).T
    bw, cw, dw = wide(grad_b), wide(grad_c), wide(grad_d)

    def weights(i, carry):
        at = pl.ds(pl.multiple_of(i * 640, 640), 640)
        cols = ut[at, :]
        grad[i, :, :, 0:40, :] = fold(dot(cols, bw)).reshape(NZ, 2, 40, 128)
        grad[i, :, :, 40:80, :] = fold(dot(cols, cw)).reshape(NZ, 2, 40, 128)
        gwd[...] = fold(dot(cols, dw))
        for s in range(16):
            third_part = jnp.concatenate([gwd[s * 40 + 32 : s * 40 + 40, :], extra], axis=0)
            packed = gwd[s * 40 : s * 40 + 16, :]
            packed = packed + pltpu.roll(gwd[s * 40 + 16 : s * 40 + 32, :], 40, 1)
            grad[i, s // 2, s % 2, 80:96, :] = packed + pltpu.roll(third_part, 80, 1)
        return carry

    lax.fori_loop(0, NX, weights, 0)
    out = fin
    cs, cr, x0s, x0r, y0s, y0r, z0s, z0r, y3s, y3r, z1s, z1r, x1s, x1r, z2s, z2r, x2s, x2r, y4s, y4r, ls, lr, ks, kr = red_sems
    keep = pl.multiple_of(core * 48, 8)
    give = pl.multiple_of((1 - core) * 48, 8)
    swap = push(grad.at[:, :, :, pl.ds(give, 48)], c_rec, cs, cr, cpeer)
    swap.start()

    bt, ctall, dtall = tall(grad_b), tall(grad_c), tall(grad_d)[:, :HEADS]
    both_t = jnp.concatenate([bt, ctall], axis=1)

    def model_grads(i, carry):
        at = pl.ds(pl.multiple_of(i * 512, 512), 512)
        both_w = jnp.concatenate([wb_ref[at, :], wc_ref[at, :]], axis=1)
        p = dot_nt(both_t, both_w) + dot_nt(dtall, wd_ref[at, :])
        gu_ref[:, at] = (p[:TOK] + p[TOK:]).astype(BF16)
        return carry

    lax.fori_loop(0, 1, model_grads, 0)
    swap.wait()
    for i in range(NX):
        h1[i] = grad[i, :, :, pl.ds(keep, 48), :] + c_rec[i]

    def part(start, there):
        return pl.ds(pl.multiple_of(start + 8 * lax.rem(there, 2), 8), 8)

    def begin(copies):
        for copy in copies:
            copy.start()
        return copies

    def arrived(copies):
        for copy in copies:
            copy.wait_recv()

    znext = [lax.rem(z + d, NZ) for d in range(1, NZ)]
    xnext = [lax.rem(x + d, NX) for d in range(1, NX)]
    z_one = begin([push(h1.at[:, t, :, pl.ds(32, 16)], c0.at[z], z0s.at[d], z0r.at[d], zpeers[d]) for d, t in enumerate(znext)])
    x_one = begin([push(h1.at[t, :, :, pl.ds(0, 16)], a0.at[x], x0s.at[d], x0r.at[d], xpeers[d]) for d, t in enumerate(xnext)])
    y_one = begin([push(h1.at[:, :, t // 2, part(16, t)], b0.at[y], y0s.at[d], y0r.at[d], ypeers[d]) for d, t in enumerate(ynext)])
    lax.fori_loop(1, 5, model_grads, 0)
    arrived(x_one)
    total = h1[x, :, :, pl.ds(0, 16), :]
    for t in xnext:
        total = total + a0[t]
    a1[...] = total
    y_two = begin([push(a1.at[:, t // 2, part(0, t)], a1r.at[y], y3s.at[d], y3r.at[d], ypeers[d]) for d, t in enumerate(ynext)])
    arrived(y_one)
    total = h1[:, :, h, part(16, yl), :]
    for t in ynext:
        total = total + b0[t]
    b1[...] = total
    z_two = begin([push(b1.at[:, t], b1r.at[z], z1s.at[d], z1r.at[d], zpeers[d]) for d, t in enumerate(znext)])
    arrived(z_one)
    total = h1[:, z, :, pl.ds(32, 16), :]
    for t in znext:
        total = total + c0[t]
    c1[...] = total
    x_two = begin([push(c1.at[t], c1r.at[x], x1s.at[d], x1r.at[d], xpeers[d]) for d, t in enumerate(xnext)])
    arrived(y_two)
    total = a1[:, h, part(0, yl), :]
    for t in ynext:
        total = total + a1r[t]
    a2[...] = total
    z_three = begin([push(a2.at[t], a2r.at[z], z2s.at[d], z2r.at[d], zpeers[d]) for d, t in enumerate(znext)])
    arrived(z_two)
    total = b1[:, z]
    for t in znext:
        total = total + b1r[t]
    b2[...] = total
    x_three = begin([push(b2.at[t], b2r.at[x], x2s.at[d], x2r.at[d], xpeers[d]) for d, t in enumerate(xnext)])
    arrived(x_two)
    total = c1[x]
    for t in xnext:
        total = total + c1r[t]
    c2[...] = total
    y_three = begin([push(c2.at[t // 2, part(0, t)], c2r.at[y], y4s.at[d], y4r.at[d], ypeers[d]) for d, t in enumerate(ynext)])
    arrived(z_three)
    total = a2[z]
    for t in znext:
        total = total + a2r[t]
    out[core, 0, yl] = total
    arrived(x_three)
    total = b2[x]
    for t in xnext:
        total = total + b2r[t]
    out[core, 1, yl] = total
    arrived(y_three)
    total = c2[h, part(0, yl), :]
    for t in ynext:
        total = total + c2r[t]
    out[core, 2, yl] = total
    last = push(out.at[core, :, yl], out.at[core, :, yl], ls, lr, lpeer)
    last.start()
    last.wait()
    both = push(out.at[core], out.at[core], ks, kr, cpeer)
    both.start()
    both.wait()

    whole = fin[...].reshape(ROWS, 128)
    gbw_ref[...] = whole[:40]
    gcw_ref[...] = whole[40:80]
    tail = whole[80:]
    gdw_ref[0:16, :] = tail[:, :HEADS]
    gdw_ref[16:32, :] = tail[:, 40:80]
    tail = tail[:, 80:120]
    gdw_ref[32:40, :] = tail[:8]
    ex_ref[...] = tail[8:]
    for c in range(CHUNKS):
        y1[c].wait_send()
        for copy in a_copies(c) + x_copies(c) + b_copies(c):
            copy.wait_send()
        y2_copy(c).wait_send()
    for copy in x_one + y_one + z_one + x_two + y_two + z_two + x_three + y_three + z_three:
        copy.wait_send()


def layer(u, x, g, wb, wc, wd, bias, alog, skip):
    vmem = pl.BlockSpec(memory_space=pltpu.VMEM)
    dma = pltpu.SemaphoreType.DMA
    half = (2, HALF, WIDTH, STATE)

    def f32(*shape):
        return pltpu.VMEM(shape + (128,), F32)

    def b16(*shape):
        return pltpu.VMEM(shape, BF16)

    def sems(counts):
        pairs = []
        for n in counts:
            pairs += [dma if n == () else dma(n)] * 2
        return pairs

    shape = jax.ShapeDtypeStruct
    return pl.pallas_call(
        layer_kernel,
        out_shape=(
            shape((TOK, MODEL), BF16), shape((TOK, MODEL), BF16), shape((40, STATE), F32),
            shape((40, STATE), F32), shape((40, HEADS), F32), shape((8, HEADS), F32),
        ),
        in_specs=[vmem] * 9,
        out_specs=(vmem,) * 6,
        scratch_shapes=[
            b16(MODEL, TOK), b16(MODEL, TOK), b16(MODEL, TOK), b16(MODEL, 256), b16(MODEL, 256),
            b16(256, 256), b16(256, 256), b16(256, 256), b16(256, 256),
            f32(TOK), f32(TOK), f32(TOK), f32(MODEL), pltpu.VMEM((256, 256), F32), pltpu.VMEM((256, 256), F32),
        ] + [f32(HEADS, 1)] * 11 + [
            f32(HEADS), f32(HEADS), f32(640),
            f32(2, HEADS, WIDTH), f32(2, 24), f32(2, HEADS, WIDTH),
            f32(*half[:3]), f32(*half[:3]),
            f32(NZ, 2, HALF, PIECE), f32(2, HALF, PIECE), f32(NX, HALF, PIECE), f32(NZ, 2, HALF, PIECE),
            f32(*half[:3]), f32(*half[:3]),
            f32(24), f32(4, 24), f32(24), f32(NZ, 24), f32(NX, 24),
            f32(NX, NZ, 2, ROWS), f32(4, 8, 2, 48), f32(4, 8, 2, 48),
            f32(4, 8, 2, 16), f32(8, 2, 16), f32(4, 8, 8), f32(8, 8), f32(8, 8),
            f32(4, 4, 8, 8), f32(4, 8, 8), f32(8, 4, 8), f32(4, 8), f32(4, 8),
            f32(8, 4, 2, 16), f32(4, 2, 16), f32(4, 2, 16), f32(2, 16), f32(4, 8),
            f32(2, 3, 2, 8),
        ] + sems(
            [(CHUNKS,), (CHUNKS, NZ - 1), (CHUNKS, NX - 1), (CHUNKS, NZ - 1), (CHUNKS,), (), (NZ - 1,), (NX - 1,)]
        ) + sems([(), (3,), (3,), (7,), (3,), (7,), (3,), (7,), (3,), (3,), (), ()]),
        compiler_params=pltpu.CompilerParams(
            collective_id=0, has_side_effects=True, vmem_limit_bytes=60 << 20
        ),
        name="layer",
    )(u, x, g, wb, wc, wd, bias, alog, skip)


def body(layer_input, ssm_input, out_grad, b_weight, c_weight, dt_weight, dt_bias, a_log, d_skip):
    gx, gu, gb, gc, gd, extra = layer(
        layer_input, ssm_input, out_grad, b_weight, c_weight, dt_weight,
        dt_bias[:, None], a_log[:, None], d_skip[:, None],
    )
    return gx, gu, gb, gc, gd, extra[0], extra[1], extra[2]


def solution(mesh):
    split_mesh = Mesh(mesh.devices.reshape(4, 8, 2, 2, 2), AXES)
    cut, whole = P(DP_SEQ, None), P()
    return jax.shard_map(
        body,
        mesh=split_mesh,
        in_specs=(cut, cut, cut) + (whole,) * 6,
        out_specs=(cut, cut) + (P(SEQ, None),) * 3 + (whole,) * 3,
        check_vma=False,
    )
```

time: 179 us -> 137 us (0.77)
  matrix products: 28.2 us -> 0 us
  local copies, waits for them, and re-layouts: 19.4 us -> 11 us
  other arithmetic: 6.81 us -> 0 us
  Pallas kernels: 123 us -> 125 us
    dot_general x18 -> x0, matrix products: 28.2 us -> none  [the longest x1 3.86 us: body(): back_in = jnp.einsum('hst,shp->thp', weight, cotangent, precision=EXACT)]
    slice x8 -> x0, local copies, waits for them, and re-layouts: 6.92 us -> none  [the longest x2 4.23 us: body(): gb = full_grads[:, :128].reshape(64, 40, 128)]
    reshape x2 -> x0, local copies, waits for them, and re-layouts: 2.2 us -> none  [the longest x1 2.12 us: body(): full_grads[:, 256:].reshape(64, 40, 40)]
    concatenate x1 -> x0, other arithmetic: 2.12 us -> none  [body(): blocks = jnp.concatenate([gb, gc, gd], axis=1).reshape(OWNERS + (ROWS, 128))]
    pallas_call x2 -> x1, Pallas kernels: 123 us -> 125 us  [layer(): pl.pallas_call(layer_kernel, out_shape=(shape((TOK, MODEL), BF16), shape(...]
    broadcast_in_dim x1 -> x3, local copies, waits for them, and re-layouts: 0.07 us -> 2.08 us  [the longest x1 0.69 us: body(): d_skip[:, None]]
    unnamed x62 -> x20, local copies, waits for them, and re-layouts: 7.84 us -> 7.62 us
where the time goes in v2:
time: 137 us; the launch traced here: 136 us
  Pallas kernels  125 us (91%)
  local copies, waits for them, and re-layouts  11 us (8%)
    pallas_call x1, Pallas kernels, layer(): pl.pallas_call(layer_kernel, out_shape=(shape((TOK, MODEL), BF16), shape(...  125 us
    unnamed x20, local copies, waits for them, and re-layouts  7.62 us

profile of v2, /device:TPU:1, one launch (start us, length us, event | category | flops | bytes accessed | tf_op | source)
XLA Modules:
  0.0 136.5 jit_solution(9174498451735304730)
XLA Ops:
  0.6 0.0 copy-start.4
  0.6 0.6 copy-done.4
  1.3 0.0 copy-start.5
  1.3 0.7 copy.18.bias_ref
  2.0 0.0 copy-done.5
  2.0 0.0 copy-start.6
  2.0 0.7 copy.19.alog_ref
  2.7 0.0 copy-done.6
  2.7 0.7 copy.20.skip_ref
  3.4 2.0 %copy.17.wd_ref = bf16[2560,40]{1,0:T(8,128)(2,1)} copy(bf16[2560,40]{0,1:T(8,128)(2,1)} %param.14) | data formatting | bytes 409600 | tf_op args[5]
  5.4 124.8 %layer.1 = (bf16[128,2560]{1,0:T(8,128)(2,1)}, bf16[128,2560]{1,0:T(8,128)(2,1)}, f32[40,128]{1,0:T(8,128)}, f32[40,128]{1,0:T(8,128)}, f32[40,40]{1,0:T(8,128)}, /*index=5*/f32[8,40]{1,0:T(8,128)}) custom-call(bf16[128,2560]{1,0:T(8,128)(2,1)} %u_ref.1, bf16[128,2560]{1,0:T(8,128)(2,1)} %x_ref.1, bf16[128,2560]{1,0:T(8,128)(2,1)} %g_ref.1, ...), custom_call_target="tpu_custom_call" | custom-call | tf_op jit(solution)/shard_map/layer/pallas_call | solution.py:603
  130.2 1.3 slice_bitcast_fusion
  131.5 0.0 copy-start
  131.5 2.0 %copy.26 = bf16[128,2560]{1,0:T(8,128)(2,1)} copy(bf16[128,2560]{1,0:T(8,128)(2,1)} %get-tuple-element.31) | data formatting | bytes 1310720
  133.6 0.0 copy-done
  133.6 0.0 copy-start.3
  133.6 0.8 copy.27
  134.4 0.0 copy-done.3
  134.4 0.0 copy-start.2
  134.4 0.6 copy.28
  135.0 0.1 copy-done.2
  135.1 0.0 copy-start.1
  135.1 0.6 copy.29
  135.7 0.1 copy-done.1
  135.9 0.6 copy.30
Async XLA Ops:
  0.6 0.7 copy-start.4
  1.3 0.7 copy-start.5
  2.0 0.7 copy-start.6
  131.5 2.0 %copy-start = (bf16[128,2560]{1,0:T(8,128)(2,1)S(1)}, bf16[128,2560]{1,0:T(8,128)(2,1)}, u32[]{:S(2)}) copy-start(bf16[128,2560]{1,0:T(8,128)(2,1)} %get-tuple-element.32) | copy-start | bytes 1966084
  133.6 0.8 copy-start.3
  134.4 0.7 copy-start.2
  135.1 0.7 copy-start.1

commit v3 on v2

--- a/solution.py
+++ b/solution.py
@@ -13,10 +13,12 @@
 MESH = pl.DeviceIdType.MESH
 HEADS, WIDTH, STATE = 40, 64, 128
 HALF = HEADS // 2
-CHUNK = 4
-CHUNKS = HALF // CHUNK
+SIZES_OF = (2, 4, 4, 4, 4, 2)
+STARTS = tuple(sum(SIZES_OF[:c]) for c in range(len(SIZES_OF)))
+CHUNKS = len(SIZES_OF)
 NX, NZ = SIZES["x"], SIZES["z"]
 PIECE = WIDTH // NZ
+FAR_FIRST = (4, 3, 5, 2, 6, 1, 7)
 
 
 def place():
@@ -46,7 +48,6 @@
 TOK = 128
 MODEL = 2560
 ROWS = 96
-BLOCK = CHUNK * WIDTH
 F32, BF16 = jnp.float32, jnp.bfloat16
 
 
@@ -104,12 +105,12 @@
     mine, other = h * HALF, (1 - h) * HALF
     partner = shifted(here, yh=1)
     cpeer = shifted(here, core=1)
-    lpeer = shifted(here, yl=1)
+    dpeers = [cpeer, shifted(here, yl=1), shifted(here, yl=1, core=1)]
     zpeers = [shifted(here, z=d) for d in range(1, NZ)]
     xpeers = [shifted(here, x=d) for d in range(1, NX)]
     ynext = [lax.rem(y + d, 4) for d in range(1, 4)]
     ypeers = [(x, z, t // 2, lax.rem(t, 2), core) for t in ynext]
-    peers = [cpeer] + ypeers + zpeers + xpeers
+    peers = [cpeer, dpeers[2]] + ypeers + zpeers + xpeers
     scan_sems, red_sems = sems[:16], sems[16:]
     y1s, y1r, as_, ar_, xss, xrs, bss, brs, y2s, y2r, d1s, d1r, d2s, d2r, d3s, d3r = scan_sems
     barrier = pltpu.get_barrier_semaphore()
@@ -117,15 +118,17 @@
         pl.semaphore_signal(barrier, inc=1, device_id=peer, device_id_type=MESH)
 
     u = u_ref[...]
-    raw = dot(u, wd_ref[...])
-    raw = jnp.concatenate([raw, jnp.zeros((TOK, TOK - HEADS), F32)], axis=1)
-    raw = raw.T[:HEADS] + bias_ref[...]
+    columns = jnp.concatenate([bias_ref[...], alog_ref[...], skip_ref[...], jnp.zeros((5, HEADS), F32)], axis=0)
+    columns = jnp.concatenate([columns, jnp.zeros((8, TOK - HEADS), F32)], axis=1)
+    columns = padded(columns).T[:HEADS]
+    alog = columns[:, 1:2]
+    raw = dot_nt(wd_ref[...], u) + columns[:, 0:1]
     small = jnp.exp(-jnp.abs(raw))
     above = 1.0 + small
     gap = above - 1.0
     log_part = jnp.where(gap == 0.0, small, jnp.log(above) * (small / jnp.where(gap == 0.0, 1.0, gap)))
     dt = jnp.maximum(raw, 0.0) + log_part
-    rate = -jnp.exp(alog_ref[...])
+    rate = -jnp.exp(alog)
     row_i = lax.broadcasted_iota(jnp.int32, (TOK, TOK), 0)
     col_i = lax.broadcasted_iota(jnp.int32, (TOK, TOK), 1)
     upto = (row_i <= col_i).astype(F32)
@@ -145,7 +148,7 @@
     rows_fs[...] = rows(from_start)
     rows_te[...] = rows(to_end)
     rows_cum[...] = rows(cum)
-    rows_skip[...] = rows(jnp.broadcast_to(skip_ref[...], (HEADS, TOK)))
+    rows_skip[...] = rows(jnp.broadcast_to(columns[:, 2:3], (HEADS, TOK)))
     decay = jnp.broadcast_to(jnp.exp(last), (HEADS, STATE))
     fill = jnp.ones((4, STATE), F32)
     dec[0] = jnp.concatenate([decay[:HALF], fill], axis=0)
@@ -155,37 +158,38 @@
     b4[...] = square(proj_b)
     c4[...] = square(proj_c)
 
-    def states(first):
-        at = pl.multiple_of(first * WIDTH, BLOCK)
-        heads = pl.ds(first, CHUNK)
-        rows_at = pl.ds(at, BLOCK)
-        xc = x_ref[:, pl.ds(at, BLOCK)].T
-        gc = g_ref[:, pl.ds(at, BLOCK)].T
+    def states(start, c):
+        count, block = SIZES_OF[c], SIZES_OF[c] * WIDTH
+        at = pl.multiple_of((start + STARTS[c]) * WIDTH, 2 * WIDTH)
+        heads = pl.ds(start + STARTS[c], count)
+        rows_at = pl.ds(at, block)
+        xc = x_ref[:, pl.ds(at, block)].T
+        gc = g_ref[:, pl.ds(at, block)].T
         xt[rows_at, :] = xc
         gt[rows_at, :] = gc
-        xsc = xc.astype(F32).reshape(CHUNK, WIDTH, TOK) * rows_ws[heads]
-        gsc = gc.astype(F32).reshape(CHUNK, WIDTH, TOK) * rows_fs[heads]
-        xwc = wide(xsc.reshape(BLOCK, TOK))
-        gwc = wide(gsc.reshape(BLOCK, TOK))
+        xsc = xc.astype(F32).reshape(count, WIDTH, TOK) * rows_ws[heads]
+        gsc = gc.astype(F32).reshape(count, WIDTH, TOK) * rows_fs[heads]
+        xwc = wide(xsc.reshape(block, TOK))
+        gwc = wide(gsc.reshape(block, TOK))
         xw[rows_at, :] = xwc
         gw[rows_at, :] = gwc
-        sr[0, heads] = fold(dot(xwc, b4[...])).reshape(CHUNK, WIDTH, STATE)
-        sr[1, heads] = fold(dot(gwc, c4[...])).reshape(CHUNK, WIDTH, STATE)
-
-    states(other)
+        sr[0, heads] = fold(dot(xwc, b4[...])).reshape(count, WIDTH, STATE)
+        sr[1, heads] = fold(dot(gwc, c4[...])).reshape(count, WIDTH, STATE)
+
+    states(other, 0)
     pl.semaphore_wait(barrier, len(peers))
     first = push(dec.at[1 - h], dpar, d1s, d1r, partner)
     first.start()
     y1 = [
         push(
-            sr.at[:, pl.ds(other + c * CHUNK, CHUNK)],
-            par.at[:, pl.ds(c * CHUNK, CHUNK)],
+            sr.at[:, pl.ds(other + STARTS[c], SIZES_OF[c])],
+            par.at[:, pl.ds(STARTS[c], SIZES_OF[c])],
             y1s.at[c], y1r.at[c], partner,
         )
         for c in range(CHUNKS)
     ]
     y1[0].start()
-    states(other + CHUNK)
+    states(other, 1)
     y1[1].start()
     xr[x] = jnp.zeros((HALF, PIECE, STATE), F32)
     first.wait()
@@ -201,9 +205,9 @@
     second = [push(pair, zd.at[z], d2s.at[d], d2r.at[d], peer) for d, peer in enumerate(zpeers)]
     for copy in second:
         copy.start()
-    states(mine)
+    states(mine, 0)
     for c in range(2, CHUNKS):
-        states(other + c * CHUNK)
+        states(other, c)
     bt4[...] = square(proj_b.T)
     ct4[...] = square(proj_c.T)
     scores[...] = jnp.where(row_i >= col_i, fold(dot(wide(proj_c), bt4[...])), 0.0)
@@ -220,7 +224,7 @@
         copy.start()
 
     def a_copies(c):
-        heads = pl.ds(c * CHUNK, CHUNK)
+        heads = pl.ds(STARTS[c], SIZES_OF[c])
         copies = []
         for d, peer in enumerate(zpeers):
             pz = pl.multiple_of(lax.rem(z + d + 1, NZ) * PIECE, PIECE)
@@ -230,7 +234,7 @@
         return copies
 
     def x_copies(c):
-        heads = pl.ds(c * CHUNK, CHUNK)
+        heads = pl.ds(STARTS[c], SIZES_OF[c])
         copies = []
         for d, peer in enumerate(xpeers):
             px = lax.rem(x + d + 1, NX)
@@ -239,7 +243,7 @@
         return copies
 
     def b_copies(c):
-        heads = pl.ds(c * CHUNK, CHUNK)
+        heads = pl.ds(STARTS[c], SIZES_OF[c])
         here_rows = pl.ds(pl.multiple_of(z * PIECE, PIECE), PIECE)
         copies = []
         for d, peer in enumerate(zpeers):
@@ -251,8 +255,8 @@
 
     def y2_copy(c):
         return push(
-            ys.at[:, pl.ds(c * CHUNK, CHUNK)],
-            car.at[:, pl.ds(mine + c * CHUNK, CHUNK)],
+            ys.at[:, pl.ds(STARTS[c], SIZES_OF[c])],
+            car.at[:, pl.ds(mine + STARTS[c], SIZES_OF[c])],
             y2s.at[c], y2r.at[c], partner,
         )
 
@@ -262,25 +266,26 @@
             y1[c + 2].start()
 
         def head(i, carry):
-            k = c * CHUNK + i
+            k = STARTS[c] + i
             at = pl.ds(k, 1)
             pq[0, k] = coef[0, at, :] * sr[0, mine + k] + coef[1, at, :] * par[0, k]
             pq[1, k] = coef[2, at, :] * sr[1, mine + k] + coef[3, at, :] * par[1, k]
             return carry
 
-        lax.fori_loop(0, CHUNK, head, 0)
-        heads = pl.ds(c * CHUNK, CHUNK)
+        lax.fori_loop(0, SIZES_OF[c], head, 0)
+        heads = pl.ds(STARTS[c], SIZES_OF[c])
         own = pl.ds(pl.multiple_of(z * PIECE, PIECE), PIECE)
         arec[z, :, heads] = pq[:, heads, own, :]
-        for copy in a_copies(c):
-            copy.start()
+        copies = a_copies(c)
+        for d in FAR_FIRST:
+            copies[d - 1].start()
 
     def totals(c):
         for copy in a_copies(c):
             copy.wait_recv()
 
         def head(i, carry):
-            k = c * CHUNK + i
+            k = STARTS[c] + i
             at = pl.ds(k, 1)
             forward = arec[0, 0, k]
             backward = arec[NZ - 1, 1, k]
@@ -291,7 +296,7 @@
             xs[1, k] = backward
             return carry
 
-        lax.fori_loop(0, CHUNK, head, 0)
+        lax.fori_loop(0, SIZES_OF[c], head, 0)
         for copy in x_copies(c):
             copy.start()
 
@@ -303,7 +308,7 @@
             copy.wait_recv()
 
         def head(i, carry):
-            k = c * CHUNK + i
+            k = STARTS[c] + i
             at = pl.ds(k, 1)
             forward = jnp.zeros((PIECE, STATE), jnp.float32)
             backward = jnp.zeros((PIECE, STATE), jnp.float32)
@@ -319,19 +324,20 @@
                 backward = zd[m, at, :] * backward + arec[m, 1, k]
             return carry
 
-        lax.fori_loop(0, CHUNK, head, 0)
-        heads = pl.ds(c * CHUNK, CHUNK)
+        lax.fori_loop(0, SIZES_OF[c], head, 0)
+        heads = pl.ds(STARTS[c], SIZES_OF[c])
         own = pl.ds(pl.multiple_of(z * PIECE, PIECE), PIECE)
         ps[:, heads, own, :] = bs[z, :, heads]
-        for copy in b_copies(c):
-            copy.start()
+        copies = b_copies(c)
+        for d in FAR_FIRST:
+            copies[d - 1].start()
 
     def finals(c):
         for copy in b_copies(c):
             copy.wait_recv()
 
         def head(i, carry):
-            k = c * CHUNK + i
+            k = STARTS[c] + i
             at = pl.ds(k, 1)
             before, after = ps[0, k], ps[1, k]
             zero = jnp.zeros_like(before)
@@ -341,7 +347,7 @@
             car[1, mine + k] = coef[0, at, :] * after + jnp.where(low, par[1, k], zero)
             return carry
 
-        lax.fori_loop(0, CHUNK, head, 0)
+        lax.fori_loop(0, SIZES_OF[c], head, 0)
         y2_copy(c).start()
 
 
@@ -368,32 +374,39 @@
     gbacc[...] = jnp.zeros((2 * TOK, 2 * TOK), F32)
     gcacc[...] = jnp.zeros((2 * TOK, 2 * TOK), F32)
 
-    def outputs(first):
-        at = pl.multiple_of(first * WIDTH, BLOCK)
-        heads = pl.ds(first, CHUNK)
-        rows_at = pl.ds(at, BLOCK)
+    def outputs(start, c):
+        count, block = SIZES_OF[c], SIZES_OF[c] * WIDTH
+        at = pl.multiple_of((start + STARTS[c]) * WIDTH, 2 * WIDTH)
+        heads = pl.ds(start + STARTS[c], count)
+        rows_at = pl.ds(at, block)
         ci = car[0, heads]
         co = car[1, heads]
         rows_cross[heads] = jnp.sum(ci * co, axis=1, keepdims=True)
-        ciw = wide(ci.reshape(BLOCK, STATE))
-        cow = wide(co.reshape(BLOCK, STATE))
-        back = fold(dot(cow, bt4[...])).reshape(CHUNK, WIDTH, TOK)
-        front = fold(dot(ciw, ct4[...])).reshape(CHUNK, WIDTH, TOK)
+        ciw = wide(ci.reshape(block, STATE))
+        cow = wide(co.reshape(block, STATE))
+        back = fold(dot(cow, bt4[...])).reshape(count, WIDTH, TOK)
+        front = fold(dot(ciw, ct4[...])).reshape(count, WIDTH, TOK)
         gbacc[...] += dot_tn(xw[rows_at, :], cow)
         gcacc[...] += dot_tn(gw[rows_at, :], ciw)
-        xf = xt[rows_at, :].astype(F32).reshape(CHUNK, WIDTH, TOK)
-        gf = gt[rows_at, :].astype(F32).reshape(CHUNK, WIDTH, TOK)
+        xf = xt[rows_at, :].astype(F32).reshape(count, WIDTH, TOK)
+        gf = gt[rows_at, :].astype(F32).reshape(count, WIDTH, TOK)
         rows_xb[heads] = jnp.sum(xf * back, axis=1, keepdims=True)
         rows_gf[heads] = jnp.sum(gf * front, axis=1, keepdims=True)
         rows_gx[heads] = jnp.sum(gf * xf, axis=1, keepdims=True)
-        total = inner[rows_at, :].reshape(CHUNK, WIDTH, TOK) + rows_te[heads] * back
+        total = inner[rows_at, :].reshape(count, WIDTH, TOK) + rows_te[heads] * back
         gx = rows_dt[heads] * total + rows_skip[heads] * gf
-        gx_ref[:, pl.ds(at, BLOCK)] = gx.reshape(BLOCK, TOK).T.astype(BF16)
-
-    within(other, 4)
+        gx_ref[:, pl.ds(at, block)] = gx.reshape(block, TOK).T.astype(BF16)
+
+    work = [(half + n, 4) for half in (other, mine) for n in range(0, HALF, 4)]
+
+    def fill(n):
+        for _ in range(min(n, len(work))):
+            within(*work.pop(0))
+
+    fill(1)
     for c in range(1, CHUNKS):
-        states(mine + c * CHUNK)
-    within(other + 4, 4)
+        states(mine, c)
+    fill(1)
     for step in range(CHUNKS + 3):
         if step < CHUNKS:
             pairs(step)
@@ -404,16 +417,18 @@
         if 0 <= step - 3 < CHUNKS:
             finals(step - 3)
         if step < 3:
-            within(other + 8 + 4 * step, 4)
+            fill(1)
+        elif step == 3:
+            fill(10)
+            outputs(mine, 0)
         else:
-            within(mine + 4 * (step - 3), 4)
-            outputs(mine + 4 * (step - 3))
+            outputs(mine, step - 3)
         if step == 5:
             for j in range(0, MODEL, 512):
                 ut[j : j + 512, :] = u_ref[:, j : j + 512].T
     for c in range(CHUNKS):
         y2_copy(c).wait_recv()
-        outputs(other + c * CHUNK)
+        outputs(other, c)
 
     sums = pairacc[...]
     sums = jnp.where(row_i >= col_i, sums, 0.0)
@@ -431,7 +446,7 @@
     dt = flat_dt[...]
     raw = flat_raw[...]
     end = flat(rows_te)
-    rate = -jnp.exp(alog_ref[...])
+    rate = -jnp.exp(alog)
     col = flat(rows_col)
     xb = end * flat(rows_xb)
     direct = col + xb
@@ -452,6 +467,13 @@
     grad_d = padded(grad_raw).T
     bw, cw, dw = wide(grad_b), wide(grad_c), wide(grad_d)
 
+    cs, cr, x0s, x0r, y0s, y0r, z0s, z0r, y3s, y3r, z1s, z1r, x1s, x1r, z2s, z2r, x2s, x2r, y4s, y4r, ls, lr = red_sems
+    keep = pl.multiple_of(core * 48, 8)
+    give = pl.multiple_of((1 - core) * 48, 8)
+
+    def swap(i):
+        return push(grad.at[i, :, :, pl.ds(give, 48)], c_rec.at[i], cs.at[i], cr.at[i], cpeer)
+
     def weights(i, carry):
         at = pl.ds(pl.multiple_of(i * 640, 640), 640)
         cols = ut[at, :]
@@ -463,29 +485,24 @@
             packed = gwd[s * 40 : s * 40 + 16, :]
             packed = packed + pltpu.roll(gwd[s * 40 + 16 : s * 40 + 32, :], 40, 1)
             grad[i, s // 2, s % 2, 80:96, :] = packed + pltpu.roll(third_part, 80, 1)
+        swap(i).start()
         return carry
 
     lax.fori_loop(0, NX, weights, 0)
     out = fin
-    cs, cr, x0s, x0r, y0s, y0r, z0s, z0r, y3s, y3r, z1s, z1r, x1s, x1r, z2s, z2r, x2s, x2r, y4s, y4r, ls, lr, ks, kr = red_sems
-    keep = pl.multiple_of(core * 48, 8)
-    give = pl.multiple_of((1 - core) * 48, 8)
-    swap = push(grad.at[:, :, :, pl.ds(give, 48)], c_rec, cs, cr, cpeer)
-    swap.start()
-
     bt, ctall, dtall = tall(grad_b), tall(grad_c), tall(grad_d)[:, :HEADS]
     both_t = jnp.concatenate([bt, ctall], axis=1)
 
     def model_grads(i, carry):
         at = pl.ds(pl.multiple_of(i * 512, 512), 512)
         both_w = jnp.concatenate([wb_ref[at, :], wc_ref[at, :]], axis=1)
-        p = dot_nt(both_t, both_w) + dot_nt(dtall, wd_ref[at, :])
+        p = dot_nt(both_t, both_w) + dot(dtall, wd_ref[:, at])
         gu_ref[:, at] = (p[:TOK] + p[TOK:]).astype(BF16)
         return carry
 
     lax.fori_loop(0, 1, model_grads, 0)
-    swap.wait()
     for i in range(NX):
+        swap(i).wait()
         h1[i] = grad[i, :, :, pl.ds(keep, 48), :] + c_rec[i]
 
     def part(start, there):
@@ -557,12 +574,9 @@
     for t in ynext:
         total = total + c2r[t]
     out[core, 2, yl] = total
-    last = push(out.at[core, :, yl], out.at[core, :, yl], ls, lr, lpeer)
-    last.start()
-    last.wait()
-    both = push(out.at[core], out.at[core], ks, kr, cpeer)
-    both.start()
-    both.wait()
+    last = begin([push(out.at[core, :, yl], out.at[core, :, yl], ls.at[d], lr.at[d], peer) for d, peer in enumerate(dpeers)])
+    for copy in last:
+        copy.wait()
 
     whole = fin[...].reshape(ROWS, 128)
     gbw_ref[...] = whole[:40]
@@ -626,7 +640,7 @@
             f32(2, 3, 2, 8),
         ] + sems(
             [(CHUNKS,), (CHUNKS, NZ - 1), (CHUNKS, NX - 1), (CHUNKS, NZ - 1), (CHUNKS,), (), (NZ - 1,), (NX - 1,)]
-        ) + sems([(), (3,), (3,), (7,), (3,), (7,), (3,), (7,), (3,), (3,), (), ()]),
+        ) + sems([(4,), (3,), (3,), (7,), (3,), (7,), (3,), (7,), (3,), (3,), (3,)]),
         compiler_params=pltpu.CompilerParams(
             collective_id=0, has_side_effects=True, vmem_limit_bytes=60 << 20
         ),
@@ -636,8 +650,8 @@
 
 def body(layer_input, ssm_input, out_grad, b_weight, c_weight, dt_weight, dt_bias, a_log, d_skip):
     gx, gu, gb, gc, gd, extra = layer(
-        layer_input, ssm_input, out_grad, b_weight, c_weight, dt_weight,
-        dt_bias[:, None], a_log[:, None], d_skip[:, None],
+        layer_input, ssm_input, out_grad, b_weight, c_weight, dt_weight.T,
+        dt_bias[None], a_log[None], d_skip[None],
     )
     return gx, gu, gb, gc, gd, extra[0], extra[1], extra[2]
 

time: 137 us -> 128 us (0.934)
  local copies, waits for them, and re-layouts: 11 us -> 6.26 us
  Pallas kernels: 125 us -> 121 us
    pallas_call x1, Pallas kernels: 125 us -> 121 us  [layer(): pl.pallas_call(layer_kernel, out_shape=(shape((TOK, MODEL), BF16), shape(...]
    unnamed x20 -> x13, local copies, waits for them, and re-layouts: 7.62 us -> 4.95 us
    broadcast_in_dim x3 -> x0, local copies, waits for them, and re-layouts: 2.08 us -> none  [the longest x1 0.69 us: body(): d_skip[:, None]]
where the time goes in v3:
time: 128 us
  Pallas kernels  121 us (95%)
  local copies, waits for them, and re-layouts  6.26 us (5%)
    pallas_call x1, Pallas kernels, layer(): pl.pallas_call(layer_kernel, out_shape=(shape((TOK, MODEL), BF16), shape(...  121 us
    unnamed x13, local copies, waits for them, and re-layouts  4.95 us

profile of v3, /device:TPU:1, one launch (start us, length us, event | category | flops | bytes accessed | tf_op | source)
XLA Modules:
  0.0 127.9 jit_solution(6731186023221991961)
XLA Ops:
  0.6 121.0 %layer.1 = (bf16[128,2560]{1,0:T(8,128)(2,1)}, bf16[128,2560]{1,0:T(8,128)(2,1)}, f32[40,128]{1,0:T(8,128)}, f32[40,128]{1,0:T(8,128)}, f32[40,40]{1,0:T(8,128)}, /*index=5*/f32[8,40]{1,0:T(8,128)}) custom-call(bf16[128,2560]{1,0:T(8,128)(2,1)} %u_ref.1, bf16[128,2560]{1,0:T(8,128)(2,1)} %x_ref.1, bf16[128,2560]{1,0:T(8,128)(2,1)} %g_ref.1, ...), custom_call_target="tpu_custom_call" | custom-call | tf_op jit(solution)/shard_map/layer/pallas_call | solution.py:617
  121.6 1.3 %slice_bitcast_fusion = (f32[40]{0:T(128)}, f32[40]{0:T(128)}, f32[40]{0:T(128)}) fusion(f32[8,40]{1,0:T(8,128)} %get-tuple-element.19), kind=kLoop, calls=%fused_computation | loop fusion | bytes 960 | tf_op jit(solution)/shard_map/squeeze | solution.py:656
  122.9 0.0 copy-start
  122.9 2.0 %copy.22 = bf16[128,2560]{1,0:T(8,128)(2,1)} copy(bf16[128,2560]{1,0:T(8,128)(2,1)} %get-tuple-element.31) | data formatting | bytes 1310720
  124.9 0.0 copy-done
  124.9 0.0 copy-start.3
  124.9 0.8 copy.23
  125.8 0.0 copy-done.3
  125.8 0.0 copy-start.2
  125.8 0.6 copy.24
  126.4 0.1 copy-done.2
  126.5 0.0 copy-start.1
  126.5 0.6 copy.25
  127.1 0.1 copy-done.1
  127.3 0.6 copy.26
Async XLA Ops:
  122.9 2.0 %copy-start = (bf16[128,2560]{1,0:T(8,128)(2,1)S(1)}, bf16[128,2560]{1,0:T(8,128)(2,1)}, u32[]{:S(2)}) copy-start(bf16[128,2560]{1,0:T(8,128)(2,1)} %get-tuple-element.32) | copy-start | bytes 1966084
  124.9 0.8 copy-start.3
  125.8 0.7 copy-start.2
  126.5 0.7 copy-start.1

commit v4 on v3

--- a/solution.py
+++ b/solution.py
@@ -47,7 +47,6 @@
 
 TOK = 128
 MODEL = 2560
-ROWS = 96
 F32, BF16 = jnp.float32, jnp.bfloat16
 
 
@@ -95,7 +94,7 @@
     xt, gt, ut, xw, gw, b4, c4, bt4, ct4, scores, pairacc, rowacc, inner, gbacc, gcacc,
     rows_dt, rows_ws, rows_fs, rows_te, rows_cum, rows_skip, rows_col, rows_xb, rows_gf, rows_cross, rows_gx,
     flat_dt, flat_raw, gwd, sr, dec, car, par, pq, arec, xs, xr, bs, ps, ys, dpar, coef, pair, zd, rd,
-    grad, c_rec, h1, a0, a1, a1r, a2, a2r, b0, b1, b1r, b2, b2r, c0, c1, c1r, c2, c2r, fin,
+    us, ur, gs, gr, h1, a0, a1, a1r, a2, a2r, b0, b1, b1r, b2, b2r, c0, c1, c1r, c2, c2r, fin,
     *sems,
 ):
     here = place()
@@ -113,6 +112,7 @@
     peers = [cpeer, dpeers[2]] + ypeers + zpeers + xpeers
     scan_sems, red_sems = sems[:16], sems[16:]
     y1s, y1r, as_, ar_, xss, xrs, bss, brs, y2s, y2r, d1s, d1r, d2s, d2r, d3s, d3r = scan_sems
+    cs, cr, x0s, x0r, y0s, y0r, z0s, z0r, y3s, y3r, z1s, z1r, x1s, x1r, z2s, z2r, x2s, x2r, y4s, y4r, ls, lr, us_sem, ur_sem = red_sems
     barrier = pltpu.get_barrier_semaphore()
     for peer in peers:
         pl.semaphore_signal(barrier, inc=1, device_id=peer, device_id_type=MESH)
@@ -189,6 +189,9 @@
         for c in range(CHUNKS)
     ]
     y1[0].start()
+    us[...] = u.astype(F32)
+    u_swap = push(us, ur, us_sem, ur_sem, cpeer)
+    u_swap.start()
     states(other, 1)
     y1[1].start()
     xr[x] = jnp.zeros((HALF, PIECE, STATE), F32)
@@ -424,8 +427,10 @@
         else:
             outputs(mine, step - 3)
         if step == 5:
+            u_swap.wait()
             for j in range(0, MODEL, 512):
-                ut[j : j + 512, :] = u_ref[:, j : j + 512].T
+                ut[j : j + 512, :TOK] = u_ref[:, j : j + 512].T
+                ut[j : j + 512, TOK:] = ur[:, j : j + 512].astype(BF16).T
     for c in range(CHUNKS):
         y2_copy(c).wait_recv()
         outputs(other, c)
@@ -465,31 +470,11 @@
     extra = jnp.where(lanes == 0, grad_bias, jnp.where(lanes == 1, grad_alog, jnp.where(lanes == 2, grad_skip, 0.0)))
     extra = padded(extra).T[:8]
     grad_d = padded(grad_raw).T
-    bw, cw, dw = wide(grad_b), wide(grad_c), wide(grad_d)
-
-    cs, cr, x0s, x0r, y0s, y0r, z0s, z0r, y3s, y3r, z1s, z1r, x1s, x1r, z2s, z2r, x2s, x2r, y4s, y4r, ls, lr = red_sems
-    keep = pl.multiple_of(core * 48, 8)
-    give = pl.multiple_of((1 - core) * 48, 8)
-
-    def swap(i):
-        return push(grad.at[i, :, :, pl.ds(give, 48)], c_rec.at[i], cs.at[i], cr.at[i], cpeer)
-
-    def weights(i, carry):
-        at = pl.ds(pl.multiple_of(i * 640, 640), 640)
-        cols = ut[at, :]
-        grad[i, :, :, 0:40, :] = fold(dot(cols, bw)).reshape(NZ, 2, 40, 128)
-        grad[i, :, :, 40:80, :] = fold(dot(cols, cw)).reshape(NZ, 2, 40, 128)
-        gwd[...] = fold(dot(cols, dw))
-        for s in range(16):
-            third_part = jnp.concatenate([gwd[s * 40 + 32 : s * 40 + 40, :], extra], axis=0)
-            packed = gwd[s * 40 : s * 40 + 16, :]
-            packed = packed + pltpu.roll(gwd[s * 40 + 16 : s * 40 + 32, :], 40, 1)
-            grad[i, s // 2, s % 2, 80:96, :] = packed + pltpu.roll(third_part, 80, 1)
-        swap(i).start()
-        return carry
-
-    lax.fori_loop(0, NX, weights, 0)
-    out = fin
+    gs[0:128, :] = jnp.where(core == 0, grad_c, grad_b)
+    gs[128:256, :] = grad_d
+    gs[256:264, :] = extra
+    cols_swap = push(gs, gr, cs, cr, cpeer)
+    cols_swap.start()
     bt, ctall, dtall = tall(grad_b), tall(grad_c), tall(grad_d)[:, :HEADS]
     both_t = jnp.concatenate([bt, ctall], axis=1)
 
@@ -500,11 +485,26 @@
         gu_ref[:, at] = (p[:TOK] + p[TOK:]).astype(BF16)
         return carry
 
-    lax.fori_loop(0, 1, model_grads, 0)
-    for i in range(NX):
-        swap(i).wait()
-        h1[i] = grad[i, :, :, pl.ds(keep, 48), :] + c_rec[i]
-
+    lax.fori_loop(0, 2, model_grads, 0)
+    cols_swap.wait()
+    both_extra = extra + gr[256:264, :]
+    main_w = wide(jnp.concatenate([jnp.where(core == 0, grad_b, grad_c), gr[0:128, :]], axis=0))
+    steps_w = wide(jnp.concatenate([grad_d, gr[128:256, :]], axis=0))
+
+    def weights(i, carry):
+        cols = ut[pl.ds(pl.multiple_of(i * 640, 640), 640), :]
+        h1[i, :, :, 0:40, :] = fold(dot(cols, main_w)).reshape(NZ, 2, 40, 128)
+        gwd[...] = fold(dot(cols, steps_w))
+        for s in range(16):
+            first_part = gwd[pl.ds(pl.multiple_of(s * 40 + 8 * core, 8), 8), :]
+            next_part = gwd[pl.ds(pl.multiple_of(s * 40 + 16 + 8 * core, 8), 8), :]
+            third_part = jnp.where(core == 0, gwd[s * 40 + 32 : s * 40 + 40, :], both_extra)
+            packed = first_part + pltpu.roll(next_part, 40, 1)
+            h1[i, s // 2, s % 2, 40:48, :] = packed + pltpu.roll(third_part, 80, 1)
+        return carry
+
+    lax.fori_loop(0, NX, weights, 0)
+    out = fin
     def part(start, there):
         return pl.ds(pl.multiple_of(start + 8 * lax.rem(there, 2), 8), 8)
 
@@ -522,7 +522,7 @@
     z_one = begin([push(h1.at[:, t, :, pl.ds(32, 16)], c0.at[z], z0s.at[d], z0r.at[d], zpeers[d]) for d, t in enumerate(znext)])
     x_one = begin([push(h1.at[t, :, :, pl.ds(0, 16)], a0.at[x], x0s.at[d], x0r.at[d], xpeers[d]) for d, t in enumerate(xnext)])
     y_one = begin([push(h1.at[:, :, t // 2, part(16, t)], b0.at[y], y0s.at[d], y0r.at[d], ypeers[d]) for d, t in enumerate(ynext)])
-    lax.fori_loop(1, 5, model_grads, 0)
+    lax.fori_loop(2, 5, model_grads, 0)
     arrived(x_one)
     total = h1[x, :, :, pl.ds(0, 16), :]
     for t in xnext:
@@ -578,10 +578,10 @@
     for copy in last:
         copy.wait()
 
-    whole = fin[...].reshape(ROWS, 128)
-    gbw_ref[...] = whole[:40]
-    gcw_ref[...] = whole[40:80]
-    tail = whole[80:]
+    whole = fin[...].reshape(2, 48, 128)
+    gbw_ref[...] = whole[0, :40]
+    gcw_ref[...] = whole[1, :40]
+    tail = jnp.concatenate([whole[0, 40:], whole[1, 40:]], axis=0)
     gdw_ref[0:16, :] = tail[:, :HEADS]
     gdw_ref[16:32, :] = tail[:, 40:80]
     tail = tail[:, 80:120]
@@ -623,7 +623,7 @@
         in_specs=[vmem] * 9,
         out_specs=(vmem,) * 6,
         scratch_shapes=[
-            b16(MODEL, TOK), b16(MODEL, TOK), b16(MODEL, TOK), b16(MODEL, 256), b16(MODEL, 256),
+            b16(MODEL, TOK), b16(MODEL, TOK), b16(MODEL, 256), b16(MODEL, 256), b16(MODEL, 256),
             b16(256, 256), b16(256, 256), b16(256, 256), b16(256, 256),
             f32(TOK), f32(TOK), f32(TOK), f32(MODEL), pltpu.VMEM((256, 256), F32), pltpu.VMEM((256, 256), F32),
         ] + [f32(HEADS, 1)] * 11 + [
@@ -633,14 +633,14 @@
             f32(NZ, 2, HALF, PIECE), f32(2, HALF, PIECE), f32(NX, HALF, PIECE), f32(NZ, 2, HALF, PIECE),
             f32(*half[:3]), f32(*half[:3]),
             f32(24), f32(4, 24), f32(24), f32(NZ, 24), f32(NX, 24),
-            f32(NX, NZ, 2, ROWS), f32(4, 8, 2, 48), f32(4, 8, 2, 48),
+            pltpu.VMEM((TOK, MODEL), F32), pltpu.VMEM((TOK, MODEL), F32), f32(264), f32(264), f32(4, 8, 2, 48),
             f32(4, 8, 2, 16), f32(8, 2, 16), f32(4, 8, 8), f32(8, 8), f32(8, 8),
             f32(4, 4, 8, 8), f32(4, 8, 8), f32(8, 4, 8), f32(4, 8), f32(4, 8),
             f32(8, 4, 2, 16), f32(4, 2, 16), f32(4, 2, 16), f32(2, 16), f32(4, 8),
             f32(2, 3, 2, 8),
         ] + sems(
             [(CHUNKS,), (CHUNKS, NZ - 1), (CHUNKS, NX - 1), (CHUNKS, NZ - 1), (CHUNKS,), (), (NZ - 1,), (NX - 1,)]
-        ) + sems([(4,), (3,), (3,), (7,), (3,), (7,), (3,), (7,), (3,), (3,), (3,)]),
+        ) + sems([(), (3,), (3,), (7,), (3,), (7,), (3,), (7,), (3,), (3,), (3,), ()]),
         compiler_params=pltpu.CompilerParams(
             collective_id=0, has_side_effects=True, vmem_limit_bytes=60 << 20
         ),

time: 128 us -> 127 us (level)
  no operation moved by 1% of the time
where the time goes in v4:
time: 127 us
  Pallas kernels  120 us (94%)
  local copies, waits for them, and re-layouts  6.26 us (5%)
    pallas_call x1, Pallas kernels, layer(): pl.pallas_call(layer_kernel, out_shape=(shape((TOK, MODEL), BF16), shape(...  120 us
    unnamed x13, local copies, waits for them, and re-layouts  4.95 us

profile of v4, /device:TPU:1, one launch (start us, length us, event | category | flops | bytes accessed | tf_op | source)
XLA Modules:
  0.0 126.8 jit_solution(3383716941552903652)
XLA Ops:
  0.6 119.9 %layer.1 = (bf16[128,2560]{1,0:T(8,128)(2,1)}, bf16[128,2560]{1,0:T(8,128)(2,1)}, f32[40,128]{1,0:T(8,128)}, f32[40,128]{1,0:T(8,128)}, f32[40,40]{1,0:T(8,128)}, /*index=5*/f32[8,40]{1,0:T(8,128)}) custom-call(bf16[128,2560]{1,0:T(8,128)(2,1)} %u_ref.1, bf16[128,2560]{1,0:T(8,128)(2,1)} %x_ref.1, bf16[128,2560]{1,0:T(8,128)(2,1)} %g_ref.1, ...), custom_call_target="tpu_custom_call" | custom-call | tf_op jit(solution)/shard_map/layer/pallas_call | solution.py:617
  120.6 1.3 %slice_bitcast_fusion = (f32[40]{0:T(128)}, f32[40]{0:T(128)}, f32[40]{0:T(128)}) fusion(f32[8,40]{1,0:T(8,128)} %get-tuple-element.19), kind=kLoop, calls=%fused_computation | loop fusion | bytes 960 | tf_op jit(solution)/shard_map/squeeze | solution.py:656
  121.9 0.0 copy-start
  121.9 2.0 %copy.22 = bf16[128,2560]{1,0:T(8,128)(2,1)} copy(bf16[128,2560]{1,0:T(8,128)(2,1)} %get-tuple-element.31) | data formatting | bytes 1310720
  123.9 0.0 copy-done
  123.9 0.0 copy-start.3
  123.9 0.8 copy.23
  124.8 0.0 copy-done.3
  124.8 0.0 copy-start.2
  124.8 0.6 copy.24
  125.4 0.1 copy-done.2
  125.5 0.0 copy-start.1
  125.5 0.6 copy.25
  126.1 0.1 copy-done.1
  126.2 0.6 copy.26
Async XLA Ops:
  121.9 2.0 %copy-start = (bf16[128,2560]{1,0:T(8,128)(2,1)S(1)}, bf16[128,2560]{1,0:T(8,128)(2,1)}, u32[]{:S(2)}) copy-start(bf16[128,2560]{1,0:T(8,128)(2,1)} %get-tuple-element.32) | copy-start | bytes 1966084
  123.9 0.8 copy-start.3
  124.8 0.7 copy-start.2
  125.5 0.7 copy-start.1

commit v5 on v4

--- a/solution.py
+++ b/solution.py
@@ -431,19 +431,21 @@
             for j in range(0, MODEL, 512):
                 ut[j : j + 512, :TOK] = u_ref[:, j : j + 512].T
                 ut[j : j + 512, TOK:] = ur[:, j : j + 512].astype(BF16).T
+    sums = pairacc[...]
+    sumw = wide(jnp.where(row_i >= col_i, sums, 0.0))
+    gbacc[...] += dot_tn(sumw, wide(dot(u_ref[...], wc_ref[...])))
+    scores[...] = fold(dot(sumw, b4[...]))
+    rowacc[...] = rowacc[...].T
     for c in range(CHUNKS):
         y2_copy(c).wait_recv()
         outputs(other, c)
 
-    sums = pairacc[...]
-    sums = jnp.where(row_i >= col_i, sums, 0.0)
-    sumw = wide(sums)
-    acc = gbacc[...] + dot_tn(sumw, wide(dot(u_ref[...], wc_ref[...])))
+    acc = gbacc[...]
     acc = acc[:TOK] + acc[TOK:]
     grad_b = fold(acc)
     acc = gcacc[...]
     acc = acc[:TOK] + acc[TOK:]
-    grad_c = fold(acc) + fold(dot(sumw, b4[...]))
+    grad_c = fold(acc) + scores[...]
 
     def flat(ref):
         return ref[...].reshape(HEADS, TOK)
@@ -458,7 +460,7 @@
     own_out = dt * xb
     own_in = flat(rows_fs) * flat(rows_gf)
     cross = flat(rows_fs)[:, TOK - 1 :] * jnp.sum(flat(rows_cross), axis=1, keepdims=True)
-    change = rowacc[...].T[:HEADS] - dt * col + own_in - own_out
+    change = rowacc[0:HEADS, :] - dt * col + own_in - own_out
     lanes = lax.broadcasted_iota(jnp.int32, (HEADS, TOK), 1)
     edge = cross + jnp.sum(own_out, axis=1, keepdims=True)
     change = change + jnp.where(lanes == TOK - 1, edge, 0.0)
@@ -491,6 +493,15 @@
     main_w = wide(jnp.concatenate([jnp.where(core == 0, grad_b, grad_c), gr[0:128, :]], axis=0))
     steps_w = wide(jnp.concatenate([grad_d, gr[128:256, :]], axis=0))
 
+    znext = [lax.rem(z + d, NZ) for d in range(1, NZ)]
+
+    def z_firsts(i):
+        copies = [
+            push(h1.at[i, n, :, pl.ds(32, 16)], c0.at[z, i], z0s.at[i, d], z0r.at[i, d], zpeers[d])
+            for d, n in enumerate(znext)
+        ]
+        return [copies[d - 1] for d in FAR_FIRST]
+
     def weights(i, carry):
         cols = ut[pl.ds(pl.multiple_of(i * 640, 640), 640), :]
         h1[i, :, :, 0:40, :] = fold(dot(cols, main_w)).reshape(NZ, 2, 40, 128)
@@ -501,6 +512,8 @@
             third_part = jnp.where(core == 0, gwd[s * 40 + 32 : s * 40 + 40, :], both_extra)
             packed = first_part + pltpu.roll(next_part, 40, 1)
             h1[i, s // 2, s % 2, 40:48, :] = packed + pltpu.roll(third_part, 80, 1)
+        for copy in z_firsts(i):
+            copy.start()
         return carry
 
     lax.fori_loop(0, NX, weights, 0)
@@ -517,9 +530,8 @@
         for copy in copies:
             copy.wait_recv()
 
-    znext = [lax.rem(z + d, NZ) for d in range(1, NZ)]
     xnext = [lax.rem(x + d, NX) for d in range(1, NX)]
-    z_one = begin([push(h1.at[:, t, :, pl.ds(32, 16)], c0.at[z], z0s.at[d], z0r.at[d], zpeers[d]) for d, t in enumerate(znext)])
+    z_one = [copy for i in range(NX) for copy in z_firsts(i)]
     x_one = begin([push(h1.at[t, :, :, pl.ds(0, 16)], a0.at[x], x0s.at[d], x0r.at[d], xpeers[d]) for d, t in enumerate(xnext)])
     y_one = begin([push(h1.at[:, :, t // 2, part(16, t)], b0.at[y], y0s.at[d], y0r.at[d], ypeers[d]) for d, t in enumerate(ynext)])
     lax.fori_loop(2, 5, model_grads, 0)
@@ -640,7 +652,7 @@
             f32(2, 3, 2, 8),
         ] + sems(
             [(CHUNKS,), (CHUNKS, NZ - 1), (CHUNKS, NX - 1), (CHUNKS, NZ - 1), (CHUNKS,), (), (NZ - 1,), (NX - 1,)]
-        ) + sems([(), (3,), (3,), (7,), (3,), (7,), (3,), (7,), (3,), (3,), (3,), ()]),
+        ) + sems([(), (3,), (3,), (NX, 7), (3,), (7,), (3,), (7,), (3,), (3,), (3,), ()]),
         compiler_params=pltpu.CompilerParams(
             collective_id=0, has_side_effects=True, vmem_limit_bytes=60 << 20
         ),

time: 127 us -> 127 us (level)
  no operation moved by 1% of the time
where the time goes in v5:
time: 127 us; the launch traced here: 126 us
  Pallas kernels  119 us (94%)
  local copies, waits for them, and re-layouts  6.26 us (5%)
    pallas_call x1, Pallas kernels, layer(): pl.pallas_call(layer_kernel, out_shape=(shape((TOK, MODEL), BF16), shape(...  119 us
    unnamed x13, local copies, waits for them, and re-layouts  4.95 us

profile of v5, /device:TPU:1, one launch (start us, length us, event | category | flops | bytes accessed | tf_op | source)
XLA Modules:
  0.0 126.3 jit_solution(1931007339416414640)
XLA Ops:
  0.6 119.4 %layer.1 = (bf16[128,2560]{1,0:T(8,128)(2,1)}, bf16[128,2560]{1,0:T(8,128)(2,1)}, f32[40,128]{1,0:T(8,128)}, f32[40,128]{1,0:T(8,128)}, f32[40,40]{1,0:T(8,128)}, /*index=5*/f32[8,40]{1,0:T(8,128)}) custom-call(bf16[128,2560]{1,0:T(8,128)(2,1)} %u_ref.1, bf16[128,2560]{1,0:T(8,128)(2,1)} %x_ref.1, bf16[128,2560]{1,0:T(8,128)(2,1)} %g_ref.1, ...), custom_call_target="tpu_custom_call" | custom-call | tf_op jit(solution)/shard_map/layer/pallas_call | solution.py:629
  120.0 1.3 %slice_bitcast_fusion = (f32[40]{0:T(128)}, f32[40]{0:T(128)}, f32[40]{0:T(128)}) fusion(f32[8,40]{1,0:T(8,128)} %get-tuple-element.19), kind=kLoop, calls=%fused_computation | loop fusion | bytes 960 | tf_op jit(solution)/shard_map/squeeze | solution.py:668
  121.3 0.0 copy-start
  121.3 2.0 %copy.22 = bf16[128,2560]{1,0:T(8,128)(2,1)} copy(bf16[128,2560]{1,0:T(8,128)(2,1)} %get-tuple-element.31) | data formatting | bytes 1310720
  123.3 0.0 copy-done
  123.3 0.0 copy-start.3
  123.3 0.8 copy.23
  124.2 0.0 copy-done.3
  124.2 0.0 copy-start.2
  124.2 0.6 copy.24
  124.8 0.1 copy-done.2
  124.9 0.0 copy-start.1
  124.9 0.6 copy.25
  125.5 0.1 copy-done.1
  125.7 0.6 copy.26
Async XLA Ops:
  121.3 2.0 %copy-start = (bf16[128,2560]{1,0:T(8,128)(2,1)S(1)}, bf16[128,2560]{1,0:T(8,128)(2,1)}, u32[]{:S(2)}) copy-start(bf16[128,2560]{1,0:T(8,128)(2,1)} %get-tuple-element.32) | copy-start | bytes 1966084
  123.3 0.8 copy-start.3
  124.2 0.7 copy-start.2
  124.9 0.7 copy-start.1

commit v6 on v5

--- a/solution.py
+++ b/solution.py
@@ -400,7 +400,7 @@
         gx = rows_dt[heads] * total + rows_skip[heads] * gf
         gx_ref[:, pl.ds(at, block)] = gx.reshape(block, TOK).T.astype(BF16)
 
-    work = [(half + n, 4) for half in (other, mine) for n in range(0, HALF, 4)]
+    work = [(other, 4)] + [(mine + n, 4) for n in range(0, HALF, 4)] + [(other + n, 4) for n in range(4, HALF, 4)]
 
     def fill(n):
         for _ in range(min(n, len(work))):
@@ -419,12 +419,8 @@
             prefixes(step - 2)
         if 0 <= step - 3 < CHUNKS:
             finals(step - 3)
-        if step < 3:
-            fill(1)
-        elif step == 3:
-            fill(10)
-            outputs(mine, 0)
-        else:
+        fill(1 if step != 2 else 2)
+        if step >= 3:
             outputs(mine, step - 3)
         if step == 5:
             u_swap.wait()

time: 127 us -> 127 us (level)
  no operation moved by 1% of the time
where the time goes in v6:
time: 127 us; the launch traced here: 126 us
  Pallas kernels  119 us (94%)
  local copies, waits for them, and re-layouts  6.26 us (5%)
    pallas_call x1, Pallas kernels, layer(): pl.pallas_call(layer_kernel, out_shape=(shape((TOK, MODEL), BF16), shape(...  119 us
    unnamed x13, local copies, waits for them, and re-layouts  4.95 us

profile of v6, /device:TPU:1, one launch (start us, length us, event | category | flops | bytes accessed | tf_op | source)
XLA Modules:
  0.0 126.3 jit_solution(11693429467173254780)
XLA Ops:
  0.6 119.3 %layer.1 = (bf16[128,2560]{1,0:T(8,128)(2,1)}, bf16[128,2560]{1,0:T(8,128)(2,1)}, f32[40,128]{1,0:T(8,128)}, f32[40,128]{1,0:T(8,128)}, f32[40,40]{1,0:T(8,128)}, /*index=5*/f32[8,40]{1,0:T(8,128)}) custom-call(bf16[128,2560]{1,0:T(8,128)(2,1)} %u_ref.1, bf16[128,2560]{1,0:T(8,128)(2,1)} %x_ref.1, bf16[128,2560]{1,0:T(8,128)(2,1)} %g_ref.1, ...), custom_call_target="tpu_custom_call" | custom-call | tf_op jit(solution)/shard_map/layer/pallas_call | solution.py:625
  120.0 1.3 %slice_bitcast_fusion = (f32[40]{0:T(128)}, f32[40]{0:T(128)}, f32[40]{0:T(128)}) fusion(f32[8,40]{1,0:T(8,128)} %get-tuple-element.19), kind=kLoop, calls=%fused_computation | loop fusion | bytes 960 | tf_op jit(solution)/shard_map/squeeze | solution.py:664
  121.3 0.0 copy-start
  121.3 2.0 %copy.22 = bf16[128,2560]{1,0:T(8,128)(2,1)} copy(bf16[128,2560]{1,0:T(8,128)(2,1)} %get-tuple-element.31) | data formatting | bytes 1310720
  123.3 0.0 copy-done
  123.3 0.0 copy-start.3
  123.3 0.8 copy.23
  124.2 0.0 copy-done.3
  124.2 0.0 copy-start.2
  124.2 0.6 copy.24
  124.8 0.1 copy-done.2
  124.9 0.0 copy-start.1
  124.9 0.6 copy.25
  125.5 0.1 copy-done.1
  125.7 0.6 copy.26
Async XLA Ops:
  121.3 2.0 %copy-start = (bf16[128,2560]{1,0:T(8,128)(2,1)S(1)}, bf16[128,2560]{1,0:T(8,128)(2,1)}, u32[]{:S(2)}) copy-start(bf16[128,2560]{1,0:T(8,128)(2,1)} %get-tuple-element.32) | copy-start | bytes 1966084
  123.3 0.8 copy-start.3
  124.2 0.7 copy-start.2
  124.9 0.7 copy-start.1

commit v7 on v6

--- a/solution.py
+++ b/solution.py
@@ -498,6 +498,15 @@
         ]
         return [copies[d - 1] for d in FAR_FIRST]
 
+    def y_firsts(i):
+        return [
+            push(
+                h1.at[i, :, n // 2, pl.ds(pl.multiple_of(16 + 8 * lax.rem(n, 2), 8), 8)], b0.at[y, i],
+                y0s.at[i, d], y0r.at[i, d], ypeers[d],
+            )
+            for d, n in enumerate(ynext)
+        ]
+
     def weights(i, carry):
         cols = ut[pl.ds(pl.multiple_of(i * 640, 640), 640), :]
         h1[i, :, :, 0:40, :] = fold(dot(cols, main_w)).reshape(NZ, 2, 40, 128)
@@ -508,7 +517,7 @@
             third_part = jnp.where(core == 0, gwd[s * 40 + 32 : s * 40 + 40, :], both_extra)
             packed = first_part + pltpu.roll(next_part, 40, 1)
             h1[i, s // 2, s % 2, 40:48, :] = packed + pltpu.roll(third_part, 80, 1)
-        for copy in z_firsts(i):
+        for copy in z_firsts(i) + y_firsts(i):
             copy.start()
         return carry
 
@@ -529,7 +538,7 @@
     xnext = [lax.rem(x + d, NX) for d in range(1, NX)]
     z_one = [copy for i in range(NX) for copy in z_firsts(i)]
     x_one = begin([push(h1.at[t, :, :, pl.ds(0, 16)], a0.at[x], x0s.at[d], x0r.at[d], xpeers[d]) for d, t in enumerate(xnext)])
-    y_one = begin([push(h1.at[:, :, t // 2, part(16, t)], b0.at[y], y0s.at[d], y0r.at[d], ypeers[d]) for d, t in enumerate(ynext)])
+    y_one = [copy for i in range(NX) for copy in y_firsts(i)]
     lax.fori_loop(2, 5, model_grads, 0)
     arrived(x_one)
     total = h1[x, :, :, pl.ds(0, 16), :]
@@ -648,7 +657,7 @@
             f32(2, 3, 2, 8),
         ] + sems(
             [(CHUNKS,), (CHUNKS, NZ - 1), (CHUNKS, NX - 1), (CHUNKS, NZ - 1), (CHUNKS,), (), (NZ - 1,), (NX - 1,)]
-        ) + sems([(), (3,), (3,), (NX, 7), (3,), (7,), (3,), (7,), (3,), (3,), (3,), ()]),
+        ) + sems([(), (3,), (NX, 3), (NX, 7), (3,), (7,), (3,), (7,), (3,), (3,), (3,), ()]),
         compiler_params=pltpu.CompilerParams(
             collective_id=0, has_side_effects=True, vmem_limit_bytes=60 << 20
         ),

time: 127 us -> 127 us (level)
  no operation moved by 1% of the time
where the time goes in v7:
time: 127 us; the launch traced here: 126 us
  Pallas kernels  120 us (94%)
  local copies, waits for them, and re-layouts  6.26 us (5%)
    pallas_call x1, Pallas kernels, layer(): pl.pallas_call(layer_kernel, out_shape=(shape((TOK, MODEL), BF16), shape(...  120 us
    unnamed x13, local copies, waits for them, and re-layouts  4.95 us

profile of v7, /device:TPU:1, one launch (start us, length us, event | category | flops | bytes accessed | tf_op | source)
XLA Modules:
  0.0 126.4 jit_solution(14646645098627992694)
XLA Ops:
  0.6 119.5 %layer.1 = (bf16[128,2560]{1,0:T(8,128)(2,1)}, bf16[128,2560]{1,0:T(8,128)(2,1)}, f32[40,128]{1,0:T(8,128)}, f32[40,128]{1,0:T(8,128)}, f32[40,40]{1,0:T(8,128)}, /*index=5*/f32[8,40]{1,0:T(8,128)}) custom-call(bf16[128,2560]{1,0:T(8,128)(2,1)} %u_ref.1, bf16[128,2560]{1,0:T(8,128)(2,1)} %x_ref.1, bf16[128,2560]{1,0:T(8,128)(2,1)} %g_ref.1, ...), custom_call_target="tpu_custom_call" | custom-call | tf_op jit(solution)/shard_map/layer/pallas_call | solution.py:634
  120.2 1.3 %slice_bitcast_fusion = (f32[40]{0:T(128)}, f32[40]{0:T(128)}, f32[40]{0:T(128)}) fusion(f32[8,40]{1,0:T(8,128)} %get-tuple-element.19), kind=kLoop, calls=%fused_computation | loop fusion | bytes 960 | tf_op jit(solution)/shard_map/squeeze | solution.py:673
  121.5 0.0 copy-start
  121.5 2.0 %copy.22 = bf16[128,2560]{1,0:T(8,128)(2,1)} copy(bf16[128,2560]{1,0:T(8,128)(2,1)} %get-tuple-element.31) | data formatting | bytes 1310720
  123.5 0.0 copy-done
  123.5 0.0 copy-start.3
  123.5 0.8 copy.23
  124.3 0.0 copy-done.3
  124.4 0.0 copy-start.2
  124.4 0.6 copy.24
  125.0 0.1 copy-done.2
  125.1 0.0 copy-start.1
  125.1 0.6 copy.25
  125.7 0.1 copy-done.1
  125.8 0.6 copy.26
Async XLA Ops:
  121.5 2.0 %copy-start = (bf16[128,2560]{1,0:T(8,128)(2,1)S(1)}, bf16[128,2560]{1,0:T(8,128)(2,1)}, u32[]{:S(2)}) copy-start(bf16[128,2560]{1,0:T(8,128)(2,1)} %get-tuple-element.32) | copy-start | bytes 1966084
  123.5 0.8 copy-start.3
  124.4 0.7 copy-start.2
  125.1 0.7 copy-start.1
